TPU v7x, 32 devices: a whole 2x2x4 slice. The times are simulated.
32 devices in a mesh: fsdp: 2 (over core), ctx: 4 (over y, x), tp: 4 (over z).
Axes of the slice: x: 2, y: 2, z: 4, core: 2. Of those that a mesh axis runs over, the one named last changes fastest.
Arguments:
- hidden: bfloat16 [4096, 768], P(('fsdp', 'ctx')), may hold values from -6 to 6
- seq_lengths: int32 [2, 4], P('fsdp'), may hold values from 1 to 2045, as said below
- norm_gain: float32 [768], replicated, may hold values from 0.1 to 1.9
- weight_x: bfloat16 [768, 1536], P(('fsdp', 'ctx'), 'tp'), may hold values from -0.21875 to 0.21875
- weight_z: bfloat16 [768, 1536], P(('fsdp', 'ctx'), 'tp'), may hold values from -0.21875 to 0.21875
- weight_bc: bfloat16 [768, 128], P(('fsdp', 'ctx')), may hold values from -0.0546875 to 0.0546875
- weight_dt: bfloat16 [768, 2, 24], P(('fsdp', 'ctx'), None, 'tp'), may hold values from -0.21875 to 0.21875
- conv_x: float32 [4, 1536], P(None, 'tp'), may hold values from -3 to 3
- conv_bc: float32 [4, 128], replicated, may hold values from -3 to 3
- dt_bias: float32 [2, 24], P(None, 'tp'), may hold values from -3 to -1
- log_rate: float32 [2, 24], P(None, 'tp'), may hold values from -5 to -1.5
- skip_scale: float32 [24], P('tp'), may hold values from 0.5 to 1.5
- gate_gain: float32 [1536], P('tp'), may hold values from 0.1 to 1.9
- weight_out: bfloat16 [1536, 768], P('tp', ('fsdp', 'ctx')), may hold values from -0.3125 to 0.3125
- cotangent: bfloat16 [4096, 768], P(('fsdp', 'ctx')), may hold values from -6 to 6
Outputs:
- out: bfloat16 [4096, 768], P(('fsdp', 'ctx'))
- grad_hidden: float32 [4096, 768], P(('fsdp', 'ctx'))
- grad_norm_gain: float32 [768], replicated
- grad_weight_x: float32 [768, 1536], P(('fsdp', 'ctx'), 'tp')
- grad_weight_z: float32 [768, 1536], P(('fsdp', 'ctx'), 'tp')
- grad_weight_bc: float32 [768, 128], P(('fsdp', 'ctx'))
- grad_weight_dt: float32 [768, 2, 24], P(('fsdp', 'ctx'), None, 'tp')
- grad_conv_x: float32 [4, 1536], P(None, 'tp')
- grad_conv_bc: float32 [4, 128], replicated
- grad_dt_bias: float32 [2, 24], P(None, 'tp')
- grad_log_rate: float32 [2, 24], P(None, 'tp')
- grad_skip_scale: float32 [24], P('tp')
- grad_gate_gain: float32 [1536], P('tp')
- grad_weight_out: float32 [1536, 768], P('tp', ('fsdp', 'ctx'))
Inputs may be any that keep to these rules, and one draw needn't show every extreme that they name: `seq_lengths`: each row holds the lengths of the 4 sequences that fill one group's 2048 tokens; in every row one sequence, at a place drawn from the seed, is longer than 1536.
All inputs are finite; a program needn't handle non-finite values.
Results may differ from a plain program's by a relative error of at most 0.018.
Values may be sent and summed in bfloat16 or wider, within the bound.
A program may use at most 64 MiB of HBM per device.

v0:
```python
from functools import partial

import jax
import jax.numpy as jnp
from jax import lax
from jax.sharding import PartitionSpec as P

SPAN = 128
INNER = 1536


epsilon = 1e-05
highest = lax.Precision.HIGHEST


def prefix(value, axis, combine, identity, reverse):
    count, place = (lax.axis_size(axis), lax.axis_index(axis))
    everything = jax.tree.map(
        lambda part, kind: lax.all_gather(part.astype(kind), axis),
        value,
        jax.tree.map(lambda a: jnp.bfloat16 if a.dtype == jnp.float32 else a.dtype, value),
    )
    start = jax.tree.map(
        lambda part, zero: jnp.broadcast_to(jnp.asarray(zero, part.dtype), part.shape),
        value,
        identity,
    )

    def lap(k, before):
        at = count - 1 - k if reverse else k
        reached = at > place if reverse else at < place
        new = combine(
            before, jax.tree.map(lambda part, own: part[at].astype(own.dtype), everything, value)
        )
        return jax.tree.map(lambda a, b: jnp.where(reached, a, b), new, before)

    return lax.fori_loop(0, count, lap, start)


def passed_along(block, axis, distance):
    devices = range(lax.axis_size(axis))
    route = [(i - distance, i) for i in devices if i - distance in devices]
    return lax.ppermute(block, axis, route)


def round_value(value):
    return lax.optimization_barrier(value.astype(jnp.bfloat16)).astype(jnp.float32)


def segment_ids(lengths_row, positions):
    seq_ends = jnp.cumsum(lengths_row)
    passed = jnp.sum((positions[:, None] >= seq_ends[None, :]).astype(jnp.int32), axis=1)
    return passed - (positions < 0).astype(jnp.int32)


def rms_norm(values, gain_row):
    return (
        values
        * lax.rsqrt(jnp.mean(values * values, axis=1, keepdims=True) + epsilon)
        * gain_row[None, :]
    )


def causal_conv(padded, kernel, seg_padded):
    kernel_len = kernel.shape[0]
    length = padded.shape[0] - kernel_len + 1
    seg_here = seg_padded[kernel_len - 1 :]
    summed = jnp.zeros((length, padded.shape[1]), jnp.float32)
    for offset in range(kernel_len):
        matching = (seg_padded[offset : offset + length] == seg_here).astype(jnp.float32)
        summed = (
            summed + padded[offset : offset + length] * kernel[offset][None, :] * matching[:, None]
        )
    return jax.nn.silu(summed)


def span_pass(carry, pieces):
    state_in, seg_prior = carry
    x_block, b_block, c_block, dt_block, decay_block, seg_block = pieces
    length = x_block.shape[0]
    cum_decay = jnp.cumsum(decay_block, axis=0)
    places = jnp.arange(length)
    below_mask = (places[:, None] > places[None, :]) & (seg_block[:, None] == seg_block[None, :])
    below_heads = below_mask[:, :, None]
    spread = cum_decay[:, None, :] - cum_decay[None, :, :]
    mixing = jnp.where(below_heads, jnp.exp(jnp.where(below_heads, spread, 0.0)), 0.0)
    scores = jnp.dot(
        c_block.astype(jnp.bfloat16),
        b_block.astype(jnp.bfloat16).T,
        preferred_element_type=jnp.float32,
    )
    weighted = x_block * dt_block[:, :, None]
    inner_part = jnp.einsum("ij,ijh,jhp->ihp", scores, mixing, weighted, precision=highest)
    reach_in = (seg_block == seg_prior).astype(jnp.float32)[:, None] * jnp.exp(cum_decay)
    carried = jnp.einsum("in,hpn,ih->ihp", c_block, state_in, reach_in, precision=highest)
    to_last = (seg_block == seg_block[length - 1]).astype(jnp.float32)[:, None] * jnp.exp(
        cum_decay[length - 1][None, :] - cum_decay
    )
    state_out = reach_in[length - 1][:, None, None] * state_in + jnp.einsum(
        "jh,jhp,jn->hpn", to_last, weighted, b_block, precision=highest
    )
    return ((state_out, seg_block[length - 1]), inner_part + carried)


def direction_pass(state_in, seg_prior, x_heads, b_rows, c_rows, step_size, log_decay, seg_rows):

    def blocks(tensor):
        return tensor.reshape((tensor.shape[0] // SPAN, SPAN) + tensor.shape[1:])

    pieces = (
        blocks(x_heads),
        blocks(b_rows),
        blocks(c_rows),
        blocks(step_size),
        blocks(log_decay),
        blocks(seg_rows),
    )
    (state_out, seg_last), outputs = lax.scan(
        jax.checkpoint(span_pass), (state_in, seg_prior), pieces
    )
    return (state_out, outputs.reshape(x_heads.shape))


def two_way(
    x_round, bc_round, dt_raw, dt_bias, log_rate, skip_scale, seg_rows, seg_before, seg_after
):
    rows_count = x_round.shape[0]
    head_count = skip_scale.shape[0]
    x_heads = x_round.reshape(rows_count, head_count, -1)
    step_size = jax.nn.softplus(dt_raw + dt_bias[None])
    log_decay = -jnp.exp(log_rate)[None] * step_size
    b_rows, c_rows = jnp.split(bc_round, 2, axis=1)
    zero_state = jnp.zeros((head_count, x_heads.shape[2], b_rows.shape[1]), jnp.float32)
    state_fwd, y_fwd = direction_pass(
        zero_state, seg_before, x_heads, b_rows, c_rows, step_size[:, 0], log_decay[:, 0], seg_rows
    )
    state_rev, y_rev = direction_pass(
        zero_state,
        seg_after,
        x_heads[::-1],
        b_rows[::-1],
        c_rows[::-1],
        step_size[::-1, 1],
        log_decay[::-1, 1],
        seg_rows[::-1],
    )
    decay_fwd = (seg_rows[rows_count - 1] == seg_before).astype(jnp.float32) * jnp.exp(
        jnp.sum(log_decay[:, 0], axis=0)
    )
    decay_rev = (seg_rows[0] == seg_after).astype(jnp.float32) * jnp.exp(
        jnp.sum(log_decay[:, 1], axis=0)
    )
    mixed = y_fwd + y_rev[::-1] + skip_scale[None, :, None] * x_heads
    return (mixed.reshape(rows_count, -1), decay_fwd, state_fwd, decay_rev, state_rev)


def carry_terms(
    bc_round, dt_raw, dt_bias, log_rate, into_fwd, into_rev, seg_rows, seg_before, seg_after
):
    step_size = jax.nn.softplus(dt_raw + dt_bias[None])
    log_decay = -jnp.exp(log_rate)[None] * step_size
    b_rows, c_rows = jnp.split(bc_round, 2, axis=1)
    reach_fwd = (seg_rows == seg_before).astype(jnp.float32)[:, None] * jnp.exp(
        jnp.cumsum(log_decay[:, 0], axis=0)
    )
    reach_rev = (seg_rows == seg_after).astype(jnp.float32)[:, None] * jnp.exp(
        jnp.cumsum(log_decay[::-1, 1], axis=0)[::-1]
    )
    y_fwd = jnp.einsum("tn,hpn,th->thp", c_rows, into_fwd, reach_fwd, precision=highest)
    y_rev = jnp.einsum("tn,hpn,th->thp", c_rows, into_rev, reach_rev, precision=highest)
    return (y_fwd + y_rev).reshape(bc_round.shape[0], -1)


def square_rows(mixed, z_proj):
    gated = mixed * jax.nn.silu(z_proj)
    return jnp.sum(gated * gated, axis=1)


def gate_norm(mixed, z_proj, gate_gain, square_total):
    gated = mixed * jax.nn.silu(z_proj)
    return gated * lax.rsqrt(square_total[:, None] / INNER + epsilon) * gate_gain[None, :]


def chain_join(earlier, later):
    return (earlier[0] * later[0], later[0][:, None, None] * earlier[1] + later[1])


def scan_upward(decay, state):
    return prefix(
        (decay, state), "ctx", chain_join, (jnp.ones_like(decay), jnp.zeros_like(state)), False
    )[1]


def scan_downward(decay, state):
    return prefix(
        (decay, state), "ctx", chain_join, (jnp.ones_like(decay), jnp.zeros_like(state)), True
    )[1]


def fetch_weights(weight_x, weight_z, weight_bc, weight_dt, weight_out):
    return (
        lax.all_gather(weight_x, ("fsdp", "ctx"), axis=0, tiled=True),
        lax.all_gather(weight_z, ("fsdp", "ctx"), axis=0, tiled=True),
        lax.all_gather(weight_bc, ("fsdp", "ctx"), axis=0, tiled=True),
        lax.all_gather(weight_dt, ("fsdp", "ctx"), axis=0, tiled=True),
        lax.all_gather(weight_out, ("fsdp", "ctx"), axis=1, tiled=True),
    )


def contract_last(left, right):
    return lax.dot_general(
        left, right, (((1,), (1,)), ((), ())), preferred_element_type=jnp.float32
    )


def contract_first(left, right):
    return lax.dot_general(
        left, right, (((0,), (0,)), ((), ())), preferred_element_type=jnp.float32
    )


def per_device(
    hidden,
    seq_lengths,
    norm_gain,
    weight_x,
    weight_z,
    weight_bc,
    weight_dt,
    conv_x,
    conv_bc,
    dt_bias,
    log_rate,
    skip_scale,
    gate_gain,
    weight_out,
    cotangent,
):
    tokens_here = hidden.shape[0]
    rim_rows = conv_x.shape[0] - 1
    first_row = lax.axis_index("ctx") * tokens_here
    positions = first_row + jnp.arange(-rim_rows, tokens_here + 1, dtype=jnp.int32)
    seg_wide = segment_ids(seq_lengths[0], positions)
    seg_padded = seg_wide[: tokens_here + rim_rows]
    seg_rows = seg_wide[rim_rows : tokens_here + rim_rows]
    seg_before = seg_wide[rim_rows - 1]
    seg_after = seg_wide[tokens_here + rim_rows]
    full_x, full_z, full_bc, full_dt, full_out = fetch_weights(
        weight_x, weight_z, weight_bc, weight_dt, weight_out
    )
    hidden_wide = hidden.astype(jnp.float32)
    normed, norm_pull = jax.vjp(rms_norm, hidden_wide, norm_gain)
    rounded = normed.astype(jnp.bfloat16)
    x_proj = jnp.dot(rounded, full_x, preferred_element_type=jnp.float32)
    z_proj = jnp.dot(rounded, full_z, preferred_element_type=jnp.float32)
    bc_proj = jnp.dot(rounded, full_bc, preferred_element_type=jnp.float32)
    dt_raw = jnp.einsum("td,dkh->tkh", rounded, full_dt, preferred_element_type=jnp.float32)
    rim_x, rim_bc = passed_along(
        (x_proj[tokens_here - rim_rows :], bc_proj[tokens_here - rim_rows :]), "ctx", 1
    )
    x_padded = jnp.concatenate([rim_x, x_proj], axis=0)
    bc_padded = jnp.concatenate([rim_bc, bc_proj], axis=0)
    conv_fn = partial(causal_conv, seg_padded=seg_padded)
    x_conv, x_conv_pull = jax.vjp(conv_fn, x_padded, conv_x)
    bc_conv, bc_conv_pull = jax.vjp(conv_fn, bc_padded, conv_bc)
    x_round = round_value(x_conv)
    bc_round = round_value(bc_conv)
    local_fn = partial(two_way, seg_rows=seg_rows, seg_before=seg_before, seg_after=seg_after)
    (own_mix, decay_fwd, state_fwd, decay_rev, state_rev), local_pull = jax.vjp(
        local_fn, x_round, bc_round, dt_raw, dt_bias, log_rate, skip_scale
    )
    into_fwd = scan_upward(decay_fwd, state_fwd)
    into_rev = scan_downward(decay_rev, state_rev)
    carry_fn = partial(carry_terms, seg_rows=seg_rows, seg_before=seg_before, seg_after=seg_after)
    carry_mix, carry_pull = jax.vjp(
        carry_fn, bc_round, dt_raw, dt_bias, log_rate, into_fwd, into_rev
    )
    mixed = own_mix + carry_mix
    square_local, square_pull = jax.vjp(square_rows, mixed, z_proj)
    square_total = lax.psum(square_local, "tp")
    normed_gate, gate_pull = jax.vjp(gate_norm, mixed, z_proj, gate_gain, square_total)
    gate_rows = normed_gate.astype(jnp.bfloat16)
    projected = jnp.dot(gate_rows, full_out, preferred_element_type=jnp.float32)
    branch_sum = lax.psum(projected.astype(jnp.bfloat16), "tp").astype(jnp.float32)
    output = (hidden_wide + branch_sum).astype(jnp.bfloat16)
    full_x, full_z, full_bc, full_dt, full_out = fetch_weights(
        weight_x, weight_z, weight_bc, weight_dt, weight_out
    )
    grad_out = contract_first(gate_rows, cotangent)
    grad_rows = contract_last(cotangent, full_out)
    grad_mixed, grad_z_gate, grad_gate_gain, grad_square = gate_pull(round_value(grad_rows))
    grad_square_total = lax.psum(grad_square, "tp")
    grad_mixed_sq, grad_z_sq = square_pull(grad_square_total)
    grad_mixed = grad_mixed + grad_mixed_sq
    grad_z_low = (grad_z_gate + grad_z_sq).astype(jnp.bfloat16)
    grad_bc_carry, grad_dt_carry, grad_bias_carry, grad_rate_carry, grad_into_fwd, grad_into_rev = (
        carry_pull(grad_mixed)
    )
    back_fwd = scan_downward(decay_fwd, grad_into_fwd)
    back_rev = scan_upward(decay_rev, grad_into_rev)
    grad_decay_fwd = jnp.sum(back_fwd * into_fwd, axis=(1, 2))
    grad_decay_rev = jnp.sum(back_rev * into_rev, axis=(1, 2))
    grad_x_round, grad_bc_local, grad_dt_local, grad_bias_local, grad_rate_local, grad_skip = (
        local_pull((grad_mixed, grad_decay_fwd, back_fwd, grad_decay_rev, back_rev))
    )
    grad_bc_total = lax.psum((grad_bc_carry + grad_bc_local).astype(jnp.bfloat16), "tp").astype(
        jnp.float32
    )
    grad_x_padded, grad_conv_x = x_conv_pull(round_value(grad_x_round))
    grad_bc_padded, grad_conv_bc = bc_conv_pull(round_value(grad_bc_total))
    back_x, back_bc = passed_along((grad_x_padded[:rim_rows], grad_bc_padded[:rim_rows]), "ctx", -1)
    grad_x_proj = grad_x_padded[rim_rows:].at[tokens_here - rim_rows :].add(back_x)
    grad_bc_proj = grad_bc_padded[rim_rows:].at[tokens_here - rim_rows :].add(back_bc)
    grad_x_low = grad_x_proj.astype(jnp.bfloat16)
    grad_bc_low = grad_bc_proj.astype(jnp.bfloat16)
    grad_dt_low = (grad_dt_carry + grad_dt_local).astype(jnp.bfloat16)
    head_part = contract_last(grad_x_low, full_x) + contract_last(grad_z_low, full_z)
    head_part = head_part + jnp.einsum(
        "tkh,dkh->td", grad_dt_low, full_dt, preferred_element_type=jnp.float32
    )
    head_sum = lax.psum(head_part.astype(jnp.bfloat16), "tp").astype(jnp.float32)
    grad_normed = head_sum + contract_last(grad_bc_low, full_bc)
    grad_hidden_norm, grad_norm_gain = norm_pull(grad_normed)
    grad_hidden = cotangent.astype(jnp.float32) + grad_hidden_norm
    grad_x = contract_first(rounded, grad_x_low)
    grad_z = contract_first(rounded, grad_z_low)
    grad_bc = contract_first(rounded, grad_bc_low)
    grad_dt = jnp.einsum("td,tkh->dkh", rounded, grad_dt_low, preferred_element_type=jnp.float32)
    shard_x, shard_z, shard_bc, shard_dt, shard_out = (
        lax.psum_scatter(
            grad_x.astype(jnp.bfloat16), ("fsdp", "ctx"), scatter_dimension=0, tiled=True
        ).astype(jnp.float32),
        lax.psum_scatter(
            grad_z.astype(jnp.bfloat16), ("fsdp", "ctx"), scatter_dimension=0, tiled=True
        ).astype(jnp.float32),
        lax.psum_scatter(
            grad_bc.astype(jnp.bfloat16), ("fsdp", "ctx"), scatter_dimension=0, tiled=True
        ).astype(jnp.float32),
        lax.psum_scatter(
            grad_dt.astype(jnp.bfloat16), ("fsdp", "ctx"), scatter_dimension=0, tiled=True
        ).astype(jnp.float32),
        lax.psum_scatter(
            grad_out.astype(jnp.bfloat16), ("fsdp", "ctx"), scatter_dimension=1, tiled=True
        ).astype(jnp.float32),
    )
    summed_small = lax.psum(
        (
            grad_norm_gain,
            grad_conv_x,
            grad_conv_bc,
            grad_bias_carry + grad_bias_local,
            grad_rate_carry + grad_rate_local,
            grad_skip,
            grad_gate_gain,
        ),
        ("fsdp", "ctx"),
    )
    return (
        output,
        grad_hidden,
        summed_small[0],
        shard_x,
        shard_z,
        shard_bc,
        shard_dt,
        summed_small[1],
        summed_small[2],
        summed_small[3],
        summed_small[4],
        summed_small[5],
        summed_small[6],
        shard_out,
    )


def solution(mesh):
    return jax.shard_map(
        per_device,
        mesh=mesh,
        in_specs=(
            P(("fsdp", "ctx"), None),
            P("fsdp", None),
            P(),
            P(("fsdp", "ctx"), "tp"),
            P(("fsdp", "ctx"), "tp"),
            P(("fsdp", "ctx"), None),
            P(("fsdp", "ctx"), None, "tp"),
            P(None, "tp"),
            P(),
            P(None, "tp"),
            P(None, "tp"),
            P("tp"),
            P("tp"),
            P("tp", ("fsdp", "ctx")),
            P(("fsdp", "ctx"), None),
        ),
        out_specs=(
            P(("fsdp", "ctx"), None),
            P(("fsdp", "ctx"), None),
            P(),
            P(("fsdp", "ctx"), "tp"),
            P(("fsdp", "ctx"), "tp"),
            P(("fsdp", "ctx"), None),
            P(("fsdp", "ctx"), None, "tp"),
            P(None, "tp"),
            P(),
            P(None, "tp"),
            P(None, "tp"),
            P("tp"),
            P("tp"),
            P("tp", ("fsdp", "ctx")),
        ),
        check_vma=False,
    )
```

profile of v0, /device:TPU:0, one launch (start us, length us, event | category | flops | bytes accessed | tf_op | source)
XLA Modules:
  0.0 888.2 jit_solution(8470622376897890651)
XLA Ops:
  9.6 25.4 %all_gather.58 = bf16[768,128]{1,0:T(8,128)(2,1)S(1)} all-gather(bf16[96,128]{1,0:T(8,128)(2,1)} %param.41), channel_id=1, replica_groups=mesh['fsdp'=2,'ctx'=4,'tp'=4] {'fsdp','ctx'}, dimensions={0}, use_global_device_ids=true | all-gather | bytes 221184 | tf_op jit(solution)/shard_map/all_gather | solution.py:204
  41.0 25.3 %all_gather.57 = bf16[768,384]{1,0:T(8,128)(2,1)S(1)} all-gather(bf16[96,384]{1,0:T(8,128)(2,1)S(1)} %copy-done.87), channel_id=1, replica_groups=mesh['fsdp'=2,'ctx'=4,'tp'=4] {'fsdp','ctx'}, dimensions={0}, use_global_device_ids=true | all-gather | bytes 663552 | tf_op jit(solution)/shard_map/all_gather | solution.py:202
  76.5 27.1 %all_gather.66 = bf16[384,768]{0,1:T(8,128)(2,1)} all-gather(bf16[384,96]{0,1:T(8,128)(2,1)S(1)} %copy-done.88), channel_id=1, replica_groups=mesh['fsdp'=2,'ctx'=4,'tp'=4] {'fsdp','ctx'}, dimensions={1}, use_global_device_ids=true | all-gather | bytes 663552 | tf_op jit(solution)/shard_map/all_gather | solution.py:206
  103.7 24.9 %all_gather.56 = bf16[768,2,6]{2,1,0:T(2,128)(2,1)S(1)} all-gather(bf16[96,2,6]{2,1,0:T(2,128)(2,1)S(1)} %copy.396), channel_id=1, replica_groups=mesh['fsdp'=2,'ctx'=4,'tp'=4] {'fsdp','ctx'}, dimensions={0}, use_global_device_ids=true | all-gather | bytes 20736 | tf_op jit(solution)/shard_map/all_gather | solution.py:205
  139.4 27.7 %all_gather.65 = bf16[768,384]{1,0:T(8,128)(2,1)} all-gather(bf16[96,384]{1,0:T(8,128)(2,1)S(1)} %copy-done.89), channel_id=1, replica_groups=mesh['fsdp'=2,'ctx'=4,'tp'=4] {'fsdp','ctx'}, dimensions={0}, use_global_device_ids=true | all-gather | bytes 663552 | tf_op jit(solution)/shard_map/all_gather | solution.py:203
  170.3 7.5 all-reduce.33
  194.8 64.1 %while.155 = (s32[]{:T(128)}, f32[6,64,64]{2,1,0:T(8,128)S(1)}, s32[]{:T(128)}, f32[4,128,6,64]{1,0,3,2:T(4,128)}, f32[4,6,64,64]{3,2,1,0:T(8,128)}, /*index=5*/...) while((s32[]{:T(128)}, f32[6,64,64]{2,1,0:T(8,128)S(1)}, ...), condition=%wide.region_8.10_spmd.clone, body=%wide.region_6.9_spmd.clone.sunk | while | flops 154003456 | bytes 2403676 | solution.py:118
  203.6 6.0 dynamic_update_slice.173
  219.6 6.0 dynamic_update_slice.173
  235.6 6.0 dynamic_update_slice.173
  251.7 6.0 dynamic_update_slice.173
  258.9 10.4 %all-gather.3 = bf16[24,64,64]{2,1,0:T(8,128)(2,1)S(1)} all-gather(bf16[6,64,64]{2,1,0:T(8,128)(2,1)S(1)} %convert_element_type.528), channel_id=5, replica_groups=mesh['fsdp'=2,'ctx'=4,'tp'=4] {'ctx'}, dimensions={0}, use_global_device_ids=true | all-gather | bytes 245760 | tf_op jit(solution)/shard_map/all_gather | solution.py:19
  276.7 60.5 %while.154 = (s32[]{:T(128)}, f32[6,64,64]{2,1,0:T(8,128)S(1)}, s32[]{:T(128)}, f32[4,128,6,64]{1,0,3,2:T(4,128)}, f32[4,6,64,64]{3,2,1,0:T(8,128)}, /*index=5*/...) while((s32[]{:T(128)}, f32[6,64,64]{2,1,0:T(8,128)S(1)}, ...), condition=%wide.region_5.7_spmd.clone, body=%wide.region_3.6_spmd.clone.sunk | while | flops 154003456 | bytes 2402164 | solution.py:118
  285.8 6.0 dynamic_update_slice.170
  300.9 6.0 dynamic_update_slice.170
  316.0 6.0 dynamic_update_slice.170
  331.2 6.0 dynamic_update_slice.170
  345.4 9.4 %all-gather.1 = bf16[24,64,64]{2,1,0:T(8,128)(2,1)S(1)} all-gather(bf16[6,64,64]{2,1,0:T(8,128)(2,1)S(1)} %convert_element_type.523), channel_id=3, replica_groups=mesh['fsdp'=2,'ctx'=4,'tp'=4] {'ctx'}, dimensions={0}, use_global_device_ids=true | all-gather | bytes 245760 | tf_op jit(solution)/shard_map/all_gather | solution.py:19
  363.9 12.4 %psum.84 = f32[512]{0:T(512)S(1)} all-reduce(f32[512]{0:T(512)S(1)} %get-tuple-element.2176), channel_id=1, replica_groups=mesh['fsdp'=2,'ctx'=4,'tp'=4] {'tp'}, use_global_device_ids=true, to_apply=%region_20.22 | all-reduce | flops 512 | bytes 4096 | tf_op jit(solution)/shard_map/psum | solution.py:280
  377.2 8.4 psum.86
  394.5 9.0 %all-gather.5 = bf16[24,64,64]{2,1,0:T(8,128)(2,1)S(1)} all-gather(bf16[6,64,64]{2,1,0:T(8,128)(2,1)S(1)} %convolution_convert_fusion.10), channel_id=7, replica_groups=mesh['fsdp'=2,'ctx'=4,'tp'=4] {'ctx'}, dimensions={0}, use_global_device_ids=true | all-gather | bytes 245760 | tf_op jit(solution)/shard_map/all_gather | solution.py:19
  404.7 10.4 %all-gather.4 = bf16[24,64,64]{2,1,0:T(8,128)(2,1)} all-gather(bf16[6,64,64]{2,1,0:T(8,128)(2,1)S(1)} %convolution_convert_fusion.11), channel_id=6, replica_groups=mesh['fsdp'=2,'ctx'=4,'tp'=4] {'ctx'}, dimensions={0}, use_global_device_ids=true | all-gather | bytes 245760 | tf_op jit(solution)/shard_map/all_gather | solution.py:19
  421.5 7.6 reduce-window.55
  433.6 116.0 %while.153 = (s32[]{:T(128)}, f32[6,64,64]{2,1,0:T(8,128)S(1)}, f32[4,128,6,64]{1,0,3,2:T(4,128)}, f32[4,128,64]{1,0,2:T(4,128)}, f32[4,128,64]{1,0,2:T(4,128)},...) while((s32[]{:T(128)}, f32[6,64,64]{2,1,0:T(8,128)S(1)}, ...), condition=%wide.region_45.47_spmd, body=%wide.region_37.46_spmd.sunk | while | flops 348644864 | bytes 5772077 | solution.py:118
  450.3 6.0 dynamic_update_slice.166
  555.6 98.8 %while.152 = (s32[]{:T(128)}, f32[6,64,64]{2,1,0:T(8,128)S(1)}, f32[4,128,6,64]{1,0,3,2:T(4,128)}, f32[4,128,64]{1,0,2:T(4,128)}, f32[4,128,64]{1,0,2:T(4,128)},...) while((s32[]{:T(128)}, f32[6,64,64]{2,1,0:T(8,128)S(1)}, ...), condition=%wide.region_34.36_spmd, body=%wide.region_26.35_spmd.sunk | while | flops 348644864 | bytes 5646909 | solution.py:118
  662.5 7.5 reduce-window.44
  704.8 12.8 %reduce-scatter.16.cloned.1.call-done = bf16[96,12]{1,0:T(8,128)(2,1)} async-done(((bf16[768,12]{1,0:T(8,128)(2,1)}), bf16[96,12]{1,0:T(8,128)(2,1)}) %reduce-scatter.16.cloned.1.call-update) | async-done | bytes 2320
  719.2 36.3 %reduce-scatter.10.cloned.1.call-done = bf16[96,384]{1,0:T(8,128)(2,1)} async-done(((bf16[768,384]{1,0:T(8,128)(2,1)}), bf16[96,384]{1,0:T(8,128)(2,1)}) %reduce-scatter.10.cloned.1.call-update) | async-done | bytes 73744 | tf_op jit(solution)/shard_map/reduce_scatter | solution.py:333
  757.1 36.3 %reduce-scatter.14.cloned.1.call-done = bf16[384,96]{0,1:T(8,128)(2,1)} async-done(((bf16[384,768]{0,1:T(8,128)(2,1)}), bf16[384,96]{0,1:T(8,128)(2,1)}) %reduce-scatter.14.cloned.1.call-update) | async-done | bytes 73744 | tf_op jit(solution)/shard_map/reduce_scatter | solution.py:342
  794.9 36.2 %reduce-scatter.8.cloned.1.call-done = bf16[96,384]{1,0:T(8,128)(2,1)} async-done(((bf16[768,384]{1,0:T(8,128)(2,1)}), bf16[96,384]{1,0:T(8,128)(2,1)}) %reduce-scatter.8.cloned.1.call-update) | async-done | bytes 73744 | tf_op jit(solution)/shard_map/reduce_scatter | solution.py:330
  844.8 27.9 %all-reduce.31 = (f32[768]{0:T(1024)}, f32[4,384]{1,0:T(4,128)}, f32[4,128]{1,0:T(4,128)}, f32[2,6]{1,0:T(2,128)}, f32[2,6]{1,0:T(2,128)}, /*index=5*/f32[6]{0:T(128)}, f32[384]{0:T(512)}) all-reduce(f32[768]{0:T(1024)S(1)} %get-tuple-element.1978, ...), channel_id=1, replica_groups=mesh['fsdp'=2,'ctx'=4,'tp'=4] {'fsdp','ctx'}, use_global_device_ids=true, to_apply=%region_56.58 | all-reduce | flops 3230 | bytes 25840 | tf_op jit(solution)/shard_map/psum | solution.py:346
  (1102 shorter events, 453.2 us)
Async XLA Ops:
  8.0 59.0 %copy-start.13 = (bf16[512,768]{1,0:T(8,128)(2,1)S(1)}, bf16[512,768]{1,0:T(8,128)(2,1)}, u32[]{:S(2)}) copy-start(bf16[512,768]{1,0:T(8,128)(2,1)} %param.36) | copy-start | bytes 2359300
  8.0 59.0 %copy-start.138 = (f32[768]{0:T(1024)S(1)}, f32[768]{0:T(1024)}, u32[]{:S(2)}) copy-start(f32[768]{0:T(1024)} %param.38) | copy-start | bytes 9220
  8.0 709.6 %reduce-scatter.16.cloned.1.call-start = ((), (), s32[]{:S(2)}) async-start(), calls=%async_computation.9 | async-start | bytes 221184
  9.5 58.2 %copy-start.99 = (f32[512]{0:T(512)}, f32[512]{0:T(512)S(1)}, u32[]{:S(2)}) copy-start(f32[512]{0:T(512)S(1)} %fusion.171) | copy-start | bytes 6148
  9.5 122.0 %copy-start.120 = (f32[512]{0:T(512)}, f32[512]{0:T(512)S(1)}, u32[]{:S(2)}) copy-start(f32[512]{0:T(512)S(1)} %fusion.224) | copy-start | bytes 6148
  37.4 143.5 %collective-permute-start.1 = (f32[3,128]{0,1:T(8,128)}, f32[3,128]{0,1:T(8,128)S(1)}, u32[]{:S(2)}, u32[]{:S(2)}) collective-permute-start(f32[3,128]{0,1:T(8,128)} %slice.335), channel_id=1, source_target_pairs={{0,4},{4,8},{8,12},{1,5},{5,9},{9,13},{2,6},{6,10},{10,14},{3,7},{... | collective-permute-start | bytes 4616 | tf_op jit(solution)/shard_map/ppermute | solution.py:43
  67.1 61.9 %copy-start.143 = (f32[2,6]{1,0:T(2,128)S(1)}, f32[2,6]{1,0:T(2,128)}, u32[]{:S(2)}) copy-start(f32[2,6]{1,0:T(2,128)} %param.46) | copy-start | bytes 148
  67.1 64.4 %copy-start.155 = (f32[2,6]{1,0:T(2,128)S(1)}, f32[2,6]{1,0:T(2,128)}, u32[]{:S(2)}) copy-start(f32[2,6]{1,0:T(2,128)} %param.45) | copy-start | bytes 148
  67.7 117.9 %copy-start.11 = (f32[512,384]{1,0:T(8,128)}, f32[512,384]{1,0:T(8,128)S(1)}, u32[]{:S(2)}) copy-start(f32[512,384]{1,0:T(8,128)S(1)} %fusion.235) | copy-start | bytes 2359300
  68.4 117.2 %collective-permute-start = (f32[3,384]{1,0:T(4,128)}, f32[3,384]{1,0:T(4,128)}, u32[]{:S(2)}, u32[]{:S(2)}) collective-permute-start(f32[3,384]{1,0:T(4,128)} %slice.329), channel_id=1, source_target_pairs={{0,4},{4,8},{8,12},{1,5},{5,9},{9,13},{2,6},{6,10},{10,14},{3,7},{... | collective-permute-start | bytes 13832 | tf_op jit(solution)/shard_map/ppermute | solution.py:43
  75.8 93.1 %copy-start.101 = (f32[512]{0:T(512)}, f32[512]{0:T(512)S(1)}, u32[]{:S(2)}) copy-start(f32[512]{0:T(512)S(1)} %get-tuple-element.2225) | copy-start | bytes 6148
  75.8 93.1 %copy-start.103 = (f32[512]{0:T(512)}, f32[512]{0:T(512)S(1)}, u32[]{:S(2)}) copy-start(f32[512]{0:T(512)S(1)} %get-tuple-element.2224) | copy-start | bytes 6148
  75.8 109.7 %copy-start.76 = (f32[512]{0:T(512)}, f32[512]{0:T(512)S(1)}, u32[]{:S(2)}) copy-start(f32[512]{0:T(512)S(1)} %get-tuple-element.2226) | copy-start | bytes 6148
  168.9 223.1 %copy-start.50 = (f32[512,6]{0,1:T(8,128)}, f32[512,6]{0,1:T(8,128)S(1)}, u32[]{:S(2)}) copy-start(f32[512,6]{0,1:T(8,128)S(1)} %exponential_multiply_fusion.6) | copy-start | bytes 36868
  273.7 81.7 %copy-start.7 = (f32[512,6,64]{0,2,1:T(8,128)}, f32[512,6,64]{0,2,1:T(8,128)S(1)}, u32[]{:S(2)}) copy-start(f32[512,6,64]{0,2,1:T(8,128)S(1)} %convolution_bitcast_fusion.12) | copy-start | bytes 2359300
  678.9 18.3 %collective-permute-start.2 = (f32[3,384]{1,0:T(4,128)}, f32[3,384]{1,0:T(4,128)}, u32[]{:S(2)}, u32[]{:S(2)}) collective-permute-start(f32[3,384]{1,0:T(4,128)} %pad_add_fusion.5), channel_id=1, source_target_pairs={{4,0},{8,4},{12,8},{5,1},{9,5},{13,9},{6,2},{10,6},{14,10},{7,3},{... | collective-permute-start | bytes 13832 | tf_op jit(solution)/shard_map/ppermute | solution.py:43
  683.4 72.1 %reduce-scatter.10.cloned.1.call-start = ((), (), s32[]{:S(2)}) async-start(), calls=%async_computation.6 | async-start | bytes 663552 | tf_op jit(solution)/shard_map/reduce_scatter | solution.py:333
  687.3 106.1 %reduce-scatter.14.cloned.1.call-start = ((), (), s32[]{:S(2)}) async-start(), calls=%async_computation.8 | async-start | bytes 663552 | tf_op jit(solution)/shard_map/reduce_scatter | solution.py:342
  693.7 137.4 %reduce-scatter.8.cloned.1.call-start = ((), (), s32[]{:S(2)}) async-start(), calls=%async_computation.5 | async-start | bytes 663552 | tf_op jit(solution)/shard_map/reduce_scatter | solution.py:330
  699.9 132.8 %all-reduce.36.cloned.1.call-start = ((), (), s32[]{:S(2)}) async-start(), calls=%async_computation.10 | async-start | bytes 3407872 | tf_op jit(solution)/shard_map/psum | solution.py:284
  703.7 128.9 %copy-start.33 = (f32[512,128]{0,1:T(8,128)S(1)}, f32[512,128]{0,1:T(8,128)}, u32[]{:S(2)}) copy-start(f32[512,128]{0,1:T(8,128)} %copy-done.32) | copy-start | bytes 786436
  703.7 128.9 %copy-start.35 = (f32[512,128]{0,1:T(8,128)S(1)}, f32[512,128]{0,1:T(8,128)}, u32[]{:S(2)}) copy-start(f32[512,128]{0,1:T(8,128)} %get-tuple-element.2179) | copy-start | bytes 786436
  703.7 128.9 %copy-start.49 = (f32[3,128]{0,1:T(8,128)S(1)}, f32[3,128]{0,1:T(8,128)}, u32[]{:S(2)}) copy-start(f32[3,128]{0,1:T(8,128)} %copy-done.48) | copy-start | bytes 4612
  703.8 128.9 %copy-start.78 = (f32[512]{0:T(512)S(1)}, f32[512]{0:T(512)}, u32[]{:S(2)}) copy-start(f32[512]{0:T(512)} %copy-done.76) | copy-start | bytes 6148
  703.8 128.9 %copy-start.81 = (f32[512]{0:T(512)S(1)}, f32[512]{0:T(512)}, u32[]{:S(2)}) copy-start(f32[512]{0:T(512)} %get-tuple-element.2227) | copy-start | bytes 6148
  703.8 128.9 %copy-start.84 = (f32[512]{0:T(512)S(1)}, f32[512]{0:T(512)}, u32[]{:S(2)}) copy-start(f32[512]{0:T(512)} %get-tuple-element.2228) | copy-start | bytes 6148
  703.8 130.2 %copy-start.131 = (f32[128]{0:T(128)S(1)}, f32[128]{0:T(128)}, u32[]{:S(2)}) copy-start(f32[128]{0:T(128)} %get-tuple-element.2235) | copy-start | bytes 1540
  703.8 130.2 %copy-start.133 = (f32[128]{0:T(128)S(1)}, f32[128]{0:T(128)}, u32[]{:S(2)}) copy-start(f32[128]{0:T(128)} %get-tuple-element.2236) | copy-start | bytes 1540
  703.8 130.2 %copy-start.135 = (f32[128]{0:T(128)S(1)}, f32[128]{0:T(128)}, u32[]{:S(2)}) copy-start(f32[128]{0:T(128)} %get-tuple-element.2237) | copy-start | bytes 1540
  703.8 130.2 %copy-start.137 = (f32[128]{0:T(128)S(1)}, f32[128]{0:T(128)}, u32[]{:S(2)}) copy-start(f32[128]{0:T(128)} %get-tuple-element.2238) | copy-start | bytes 1540
  703.9 175.4 %reduce-scatter.12.cloned.1.call-start = ((), (), s32[]{:S(2)}) async-start(), calls=%async_computation.7 | async-start | bytes 221184 | tf_op jit(solution)/shard_map/reduce_scatter | solution.py:336
  834.7 6.2 collective-permute-start.3
  (160 other events, 1762.4 us)
Sparse Core Ops, SparseCore 0:
  683.5 34.0 reduce-scatter.15
  721.1 34.3 reduce-scatter.9
  758.9 34.3 reduce-scatter.13
  796.6 34.3 reduce-scatter.7
  844.9 34.3 reduce-scatter.11
Sparse Core Ops, SparseCore 1:
  703.9 74.4 all-reduce.35
where the time goes:
time: 903 us; the launch traced here: 888 us
  local copies, waits for them, and re-layouts  278 us (31%)
  blocking collectives  226 us (25%)
  waiting for transfers between devices  130 us (14%)
  other arithmetic  114 us (13%)
  matrix products  103 us (11%)
  between operations  20.8 us (2%)
  starting transfers between devices  10.8 us (1%)
    dynamic_update_slice x56, local copies, waits for them, and re-layouts, direction_pass(): lax.scan(jax.checkpoint(span_pass), (state_in, seg_prior), pieces)  133 us
    squeeze x56, local copies, waits for them, and re-layouts, direction_pass(): lax.scan(jax.checkpoint(span_pass), (state_in, seg_prior), pieces)  42.7 us
    all_gather x4, blocking collectives, prefix(): lax.all_gather(part.astype(kind), axis)  39.2 us
    reduce_scatter x1, waiting for transfers between devices, per_device(): lax.psum_scatter(grad_z.astype(jnp.bfloat16), ('fsdp', 'ctx'), scatter_di...  36.3 us
    reduce_scatter x1, waiting for transfers between devices, per_device(): lax.psum_scatter(grad_out.astype(jnp.bfloat16), ('fsdp', 'ctx'), scatter_...  36.3 us
    reduce_scatter x1, waiting for transfers between devices, per_device(): lax.psum_scatter(grad_x.astype(jnp.bfloat16), ('fsdp', 'ctx'), scatter_di...  36.2 us
    dot_general x24, matrix products, span_pass(): jnp.einsum('ij,ijh,jhp->ihp', scores, mixing, weighted, precision=highest)  29.8 us
    psum x1, blocking collectives, per_device(): lax.psum((grad_norm_gain, grad_conv_x, grad_conv_bc, grad_bias_carry + gr...  27.9 us
  transfers between devices with their start and end apart: 10, of which 6 were waited for; matrix products, arithmetic and copies ran while one was open for 6% of the time, Pallas kernels for 0%

commit v1 on v0

v1 whole, which is shorter than its diff:
```python
from functools import partial

import jax
import jax.numpy as jnp
from jax import lax
from jax.experimental import pallas as pl
from jax.experimental.pallas import tpu as pltpu
from jax.sharding import PartitionSpec as P

MESH = pl.DeviceIdType.MESH
F32 = jnp.float32
BF16 = jnp.bfloat16
EPS = 1e-05
TB = 128


def mm(left, right):
    return lax.dot_general(left, right, (((1,), (0,)), ((), ())), preferred_element_type=F32)


def mm_nt(left, right):
    return lax.dot_general(left, right, (((1,), (1,)), ((), ())), preferred_element_type=F32)


def mm_tn(left, right):
    return lax.dot_general(left, right, (((0,), (0,)), ((), ())), preferred_element_type=F32)


def split3(value):
    high = value.astype(BF16)
    rest = value - high.astype(F32)
    middle = rest.astype(BF16)
    low = (rest - middle.astype(F32)).astype(BF16)
    return high, middle, low


def exact_left(ones, value, dot=mm):
    a, b, c = split3(value)
    return dot(ones, a) + dot(ones, b) + dot(ones, c)


def exact_right(value, ones, dot=mm):
    a, b, c = split3(value)
    return dot(a, ones) + dot(b, ones) + dot(c, ones)


def iota(shape, dim):
    return lax.broadcasted_iota(jnp.int32, shape, dim)


def mixer_kernel(dims, *refs):
    (lens, hid, gain, wsh, kc, hrow, prow, cot, out, gh, gwx, gwz, gwbc, gwdt, gwo, small, hbuf, nl,
     wbuf, xp, dtr, u, low, z, ggate, ld, cc, cct, dte, rea, tol, w16, q16, gm, gmt, pexp, yfr, s16,
     sbuf, dec, decbuf, into16, gated, mixed, dmix, dy, st, stbuf, gall, glow, ob, obuf, oag, hb,
     hpbuf, hag, rdy, d16, dbuf, back16, dg, dw, dcc, ddt, du, gw16, fbuf, hsend, cbuf, bcs, bcbuf,
     sm, smbuf, ssem, rsem) = refs
    nf, nc, nt, hl = dims
    tok, width = hid.shape
    rows_w = wsh.shape[0]
    inner = prow.shape[1]
    pdim = inner // hl
    conv_w = inner + 128
    p1 = inner + 256
    nb = tok // TB
    taps = 4
    f, c, t = lax.axis_index("fsdp"), lax.axis_index("ctx"), lax.axis_index("tp")
    base = c * tok
    counter = [0]

    def remote(src, dst, dev):
        i = counter[0]
        counter[0] += 1
        copy = pltpu.make_async_remote_copy(
            src_ref=src, dst_ref=dst, send_sem=ssem.at[i], recv_sem=rsem.at[i],
            device_id=dev, device_id_type=MESH,
        )
        copy.start()
        return copy

    def fs(k):
        return (lax.rem(f + k, nf), c, t)

    def cx(k):
        return (f, lax.rem(c + k, nc), t)

    def tx(k):
        return (f, c, lax.rem(t + k, nt))

    pending = []

    barrier = pltpu.get_barrier_semaphore()
    peers = [fs(k) for k in range(1, nf)] + [cx(k) for k in range(1, nc)] + [tx(k) for k in range(1, nt)]
    for dev in peers:
        pl.semaphore_signal(barrier, inc=1, device_id=dev, device_id_type=MESH)
    pl.semaphore_wait(barrier, len(peers))

    me = f * nc + c
    col_parts = (pl.ds(0, p1), pl.ds(p1, 2 * inner))
    rim = remote(hid.at[pl.ds(tok - 16, 16)], hbuf, cx(1))
    ctx_copies = []
    fwd_copies = []
    for cols in col_parts:
        ctx_copies.append(
            [remote(wsh.at[:, cols], wbuf.at[me, :, cols], cx(k)) for k in range(1, nc)]
        )
        fwd_copies.append(
            [remote(wsh.at[:, cols], wbuf.at[me, :, cols], fs(k)) for k in range(1, nf)]
        )
    wbuf[me] = wsh[...]

    gain_row = gain[...]

    def norm_low(rows):
        h = rows.astype(F32)
        r = lax.rsqrt(jnp.mean(h * h, axis=1, keepdims=True) + EPS)
        return (h * r * gain_row).astype(BF16)

    @pl.loop(0, nb)
    def _(i):
        at = pl.multiple_of(i * TB, TB)
        nl[pl.ds(16 + at, TB), :] = norm_low(hid[pl.ds(at, TB), :])

    ends = []
    total = lens[0, 0]
    ends.append(total)
    for k in range(1, lens.shape[1]):
        total = total + lens[0, k]
        ends.append(total)

    def seg_of(pos):
        seg = jnp.where(pos < 0, -1, 0)
        for e in ends:
            seg = seg + jnp.where(pos >= e, 1, 0)
        return seg

    one_pos = jnp.full((1, 1), 0, jnp.int32)
    seg_before = seg_of(one_pos + (base - 1))
    seg_first = seg_of(one_pos + base)
    seg_last = seg_of(one_pos + (base + tok - 1))
    seg_after = seg_of(one_pos + (base + tok))
    seg_row = seg_of(iota((1, tok), 1) + base)
    place_row = iota((1, tok), 1)

    def seg_col(start, count, shift=0):
        return seg_of(iota((count, 1), 0) + (base + start + shift))

    def receive_weights(part):
        cols = col_parts[part]
        later = []
        for k in range(1, nc):
            ctx_copies[part][k - 1].wait_recv()
            src = f * nc + lax.rem(c + nc - k, nc)
            for j in range(1, nf):
                later.append(remote(wbuf.at[src, :, cols], wbuf.at[src, :, cols], fs(j)))
        for copy in fwd_copies[part] + later:
            copy.wait_recv()
        pending.extend(ctx_copies[part] + fwd_copies[part] + later)

    def weights(lo, hi):
        if rows_w % 16 == 0:
            return wbuf[:, :, lo:hi].reshape(width, hi - lo)
        return wbuf[:, :, lo:hi].astype(F32).reshape(width, hi - lo).astype(BF16)

    rim.wait_recv()
    pending.append(rim)
    nl[0:16, :] = norm_low(hbuf[...])
    receive_weights(0)

    w1 = weights(0, p1)
    head = mm(nl[0:16, :], w1)
    xp[0:16, :] = head[:, :conv_w]
    for i in range(tok // 256):
        got = mm(nl[16 + i * 256 : 16 + (i + 1) * 256, :], w1)
        xp[16 + i * 256 : 16 + (i + 1) * 256, :] = got[:, :conv_w]
        dtr[i * 256 : (i + 1) * 256, :] = got[:, conv_w:] + hrow[0:1, :]

    for i in range(nb):
        lo = i * TB
        here = seg_col(lo, TB)
        acc = xp[16 + lo : 16 + lo + TB, :] * kc[taps - 1 : taps, :]
        for d in range(1, taps):
            match = (seg_col(lo, TB, -d) == here).astype(F32)
            acc = acc + xp[16 + lo - d : 16 + lo - d + TB, :] * kc[taps - 1 - d : taps - d, :] * match
        u[lo : lo + TB, :] = acc
        low[lo : lo + TB, :] = (acc * jax.nn.sigmoid(acc)).astype(BF16)

    lane = iota((1, 128), 1)
    is_fwd = lane < hl
    rate_row = -jnp.exp(hrow[1:2, :])
    raw = dtr[...]
    step = jnp.maximum(raw, 0.0) + jnp.log1p(jnp.exp(-jnp.abs(raw)))
    decay = step * rate_row
    ld[...] = decay
    tri = (iota((tok, tok), 0) >= iota((tok, tok), 1)).astype(F32).astype(BF16)
    sums = exact_left(tri, decay)
    tot = sums[tok - 1 : tok, :]
    cum = jnp.where(is_fwd, sums, tot - sums + decay)
    cc[...] = cum
    cct[...] = cum.T
    dec_mask = jnp.where(
        is_fwd,
        (seg_last == seg_before).astype(F32),
        (seg_first == seg_after).astype(F32),
    )
    dec_row = jnp.exp(tot) * dec_mask
    dec[...] = jnp.broadcast_to(dec_row, (8, 128))
    dec_copies = [remote(dec, decbuf.at[k - 1], cx(k)) for k in range(1, nc)]

    spread = (
        iota((128, 2 * inner), 0) == lax.div(iota((128, 2 * inner), 1), pdim)
    ).astype(F32).astype(BF16)
    seg_all = seg_col(0, tok)
    reach = jnp.exp(cum) * jnp.where(
        is_fwd, (seg_all == seg_before).astype(F32), (seg_all == seg_after).astype(F32)
    )
    to_end = jnp.exp(tot - cum) * jnp.where(
        is_fwd, (seg_all == seg_last).astype(F32), (seg_all == seg_first).astype(F32)
    )
    rea[...] = exact_right(reach, spread)
    tol[...] = exact_right(to_end, spread)
    dte[...] = exact_right(step, spread)

    @pl.loop(0, nb)
    def _(i):
        rows = pl.ds(pl.multiple_of(i * TB, TB), TB)
        x = low[rows, :inner].astype(F32)
        w = (jnp.concatenate([x, x], axis=1) * dte[rows, :]).astype(BF16)
        w16[rows, :] = w
        q16[rows, :] = (w.astype(F32) * tol[rows, :]).astype(BF16)

    state_n = 64
    b16 = low[:, inner : inner + state_n]
    c16 = low[:, inner + state_n :]
    s16[...] = mm_tn(b16, q16[...]).astype(BF16)

    def half_of(forward):
        return pl.ds(pl.multiple_of(jnp.where(forward, 0, inner), 128), inner)

    state_copies = []
    for k in range(1, nc):
        forward = lax.rem(c + k, nc) > c
        state_copies.append(remote(s16.at[:, half_of(forward)], sbuf.at[k - 1], cx(k)))

    local = iota((TB, TB), 0)
    below = local > iota((TB, TB), 1)
    above = local < iota((TB, TB), 1)
    pair_left = iota((1, 128), 1) < pdim

    def mix_mask(i):
        same = seg_col(i * TB, TB) == seg_row
        return same & (iota((TB, 1), 0) + i * TB != place_row)

    for i in range(nb):
        lo, hi = i * TB, (i + 1) * TB
        mask = mix_mask(i)
        g = jnp.where(mask, mm_nt(c16[lo:hi], b16), 0.0)
        gm[lo:hi, :] = g
        gmt[lo:hi, :] = jnp.where(mask, mm_nt(b16[lo:hi], c16), 0.0)

    for i in range(nb):
        lo, hi = i * TB, (i + 1) * TB
        g_diag = gm[lo:hi, lo:hi]
        g_low = jnp.where(below, g_diag, 0.0)
        g_up = jnp.where(above, g_diag, 0.0)
        for pair in range(hl // 2):
            cols = slice(pair * 128, (pair + 1) * 128)
            cols_r = slice(inner + pair * 128, inner + (pair + 1) * 128)
            ys = []
            for h in (2 * pair, 2 * pair + 1):
                fc = cc[lo:hi, h : h + 1]
                rc = cc[lo:hi, hl + h : hl + h + 1]
                fr = cct[h : h + 1, :]
                rr = cct[hl + h : hl + h + 1, :]
                p = jnp.exp(jnp.minimum(fc - fr[:, lo:hi], rc - rr[:, lo:hi]))
                pexp[h, lo:hi, lo:hi] = p.astype(BF16)
                lows = [(g_low * p).astype(BF16)]
                ups = [(g_up * p).astype(BF16)]
                if i > 0:
                    p = jnp.exp(fc - fr[:, :lo])
                    pexp[h, lo:hi, :lo] = p.astype(BF16)
                    lows.insert(0, (gm[lo:hi, :lo] * p).astype(BF16))
                if i < nb - 1:
                    p = jnp.exp(rc - rr[:, hi:])
                    pexp[h, lo:hi, hi:] = p.astype(BF16)
                    ups.append((gm[lo:hi, hi:] * p).astype(BF16))
                lows = jnp.concatenate(lows, axis=1) if len(lows) > 1 else lows[0]
                ups = jnp.concatenate(ups, axis=1) if len(ups) > 1 else ups[0]
                ys.append((mm(lows, w16[:hi, cols]), mm(ups, w16[lo:, cols_r])))
            yfr[lo:hi, cols] = jnp.where(pair_left, ys[0][0], ys[1][0])
            yfr[lo:hi, cols_r] = jnp.where(pair_left, ys[0][1], ys[1][1])

    receive_weights(1)
    wz = weights(p1, p1 + inner)
    wo = weights(p1 + inner, p1 + 2 * inner)
    for i in range(tok // 256):
        rows = slice(i * 256, (i + 1) * 256)
        z[rows, :] = mm(nl[16 + i * 256 : 16 + (i + 1) * 256, :], wz)
        ggate[rows, :] = mm(cot[rows, :], wo).astype(BF16)

    dec_spread = []
    for k in range(1, nc):
        dec_copies[k - 1].wait_recv()
        dec_spread.append(exact_right(decbuf[k - 1], spread)[0:1, :])
    pending.extend(dec_copies)
    for copy in state_copies:
        copy.wait_recv()
    pending.extend(state_copies)
    acc_f = jnp.zeros((state_n, inner), F32)
    acc_r = jnp.zeros((state_n, inner), F32)
    for k in range(nc - 1, 0, -1):
        new = dec_spread[k - 1][:, :inner] * acc_f + sbuf[k - 1].astype(F32)
        acc_f = jnp.where(k <= c, new, acc_f)
    for k in range(1, nc):
        new = dec_spread[k - 1][:, inner:] * acc_r + sbuf[k - 1].astype(F32)
        acc_r = jnp.where(k > c, new, acc_r)
    into16[:, :inner] = acc_f.astype(BF16)
    into16[:, inner:] = acc_r.astype(BF16)

    skip_row = prow[0:1, :]
    gain_gate = prow[1:2, :]
    row_s = (iota((8, inner), 0) == 0).astype(F32).astype(BF16)
    row_t = (iota((8, inner), 0) == 1).astype(F32).astype(BF16)

    for i in range(nb):
        rows = slice(i * TB, (i + 1) * TB)
        carried = mm(low[rows, inner + state_n :], into16[...]) * rea[rows, :]
        y = yfr[rows, :] + carried
        yfr[rows, :] = y
        mix = y[:, :inner] + y[:, inner:] + skip_row * low[rows, :inner].astype(F32)
        mixed[rows, :] = mix
        zz = z[rows, :]
        gt = mix * zz * jax.nn.sigmoid(zz)
        gated[rows, :] = gt
        s = exact_left(row_s, gt * gt, mm_nt)
        s = s + exact_left(row_t, ggate[rows, :].astype(F32) * gain_gate * gt, mm_nt)
        st[:, rows] = s
    st_copies = [remote(st, stbuf.at[k - 1], tx(k)) for k in range(1, nt)]
    rows_sum = st[...]
    for k in range(1, nt):
        st_copies[k - 1].wait_recv()
        rows_sum = rows_sum + stbuf[k - 1]
    pending.extend(st_copies)
    total_inner = inner * nt
    r_row = lax.rsqrt(rows_sum[0:1, :] * (1.0 / total_inner) + EPS)
    q_row = r_row * r_row * r_row * rows_sum[1:2, :] * (-1.0 / total_inner)
    row8 = iota((8, tok), 0)
    rq = jnp.where(row8 == 0, r_row, jnp.where(row8 == 1, q_row, 0.0))
    pick = (iota((8, 256), 0) == lax.div(iota((8, 256), 1), 128)).astype(F32).astype(BF16)
    rq_cols = exact_right(rq, pick, mm_tn)

    acc_gain = jnp.zeros((1, inner), F32)
    acc_skip = jnp.zeros((1, inner), F32)
    for i in range(nb):
        rows = slice(i * TB, (i + 1) * TB)
        r = rq_cols[rows, 0:1]
        q = rq_cols[rows, 128:129]
        gt = gated[rows, :]
        gg = ggate[rows, :].astype(F32)
        ghat = gt * r
        glow[rows, :] = (ghat * gain_gate).astype(BF16)
        acc_gain = acc_gain + jnp.sum(gg * ghat, axis=0, keepdims=True)
        ggated = gg * gain_gate * r + gt * q
        zz = z[rows, :]
        sg = jax.nn.sigmoid(zz)
        dm = ggated * zz * sg
        mix = mixed[rows, :]
        gall[rows, p1:] = (ggated * mix * (sg * (1.0 + zz * (1.0 - sg)))).astype(BF16)
        dmix[rows, :] = dm
        acc_skip = acc_skip + jnp.sum(dm * low[rows, :inner].astype(F32), axis=0, keepdims=True)
        d = dm.astype(BF16)
        dy[rows, :] = d
        rdy[rows, :] = (jnp.concatenate([d, d], axis=1).astype(F32) * rea[rows, :]).astype(BF16)
    d16[...] = mm_tn(low[:, inner + state_n :], rdy[...]).astype(BF16)
    back_copies = []
    for k in range(1, nc):
        forward = lax.rem(c + k, nc) < c
        back_copies.append(remote(d16.at[:, half_of(forward)], dbuf.at[k - 1], cx(k)))

    for i in range(tok // 256):
        rows = slice(i * 256, (i + 1) * 256)
        ob[rows, :] = mm_nt(glow[rows, :], wo).astype(BF16)
    chunk = tok // nt

    def spread_chunks(src, dst):
        copies = []
        for k in range(1, nt):
            at = pl.multiple_of(lax.rem(t + k, nt) * chunk, chunk)
            copies.append(remote(src.at[pl.ds(at, chunk)], dst.at[k - 1], tx(k)))
        return copies

    def gather_chunks(src, dst, total, copies):
        own = pl.ds(pl.multiple_of(t * chunk, chunk), chunk)
        acc = src[own, :].astype(F32)
        for k in range(1, nt):
            copies[k - 1].wait_recv()
            acc = acc + dst[k - 1].astype(F32)
        pending.extend(copies)
        total[own, :] = acc.astype(BF16)
        return [remote(total.at[own], total.at[own], tx(k)) for k in range(1, nt)]

    out_copies = spread_chunks(ob, obuf)

    col_sets = ((0, p1), (p1, p1 + 2 * inner))

    def send_grads(part):
        lo, hi = col_sets[part]
        copies = []
        for k in range(1, nf):
            to = pl.ds(lax.rem(f + k, nf) * nc, nc)
            copies.append(
                remote(gw16.at[to, :, pl.ds(lo, hi - lo)], fbuf.at[k - 1, :, :, pl.ds(lo, hi - lo)], fs(k))
            )
        return copies

    def pass_grads(part, copies):
        lo, hi = col_sets[part]
        for copy in copies:
            copy.wait_recv()
        pending.extend(copies)
        onward = []
        for k in range(nc):
            to = lax.rem(c + k, nc)
            acc = gw16[f * nc + to, :, lo:hi].astype(F32)
            for j in range(1, nf):
                acc = acc + fbuf[j - 1, to, :, lo:hi].astype(F32)
            hsend[k, :, lo:hi] = acc.astype(BF16)
            if k > 0:
                onward.append(
                    remote(hsend.at[k, :, pl.ds(lo, hi - lo)], cbuf.at[k - 1, :, pl.ds(lo, hi - lo)], cx(k))
                )
        return onward

    def finish_grads(part, onward):
        lo, hi = col_sets[part]
        for copy in onward:
            copy.wait_recv()
        pending.extend(onward)
        acc = hsend[0, :, lo:hi].astype(F32)
        for k in range(1, nc):
            acc = acc + cbuf[k - 1, :, lo:hi].astype(F32)
        return acc

    block = 384
    per = block // rows_w

    def store_grads(b, lo, hi, value):
        for s in range(per):
            gw16[b * per + s, :, lo:hi] = value[s * rows_w : (s + 1) * rows_w].astype(BF16)

    for b in range(width // block):
        cols = slice(b * block, (b + 1) * block)
        store_grads(b, p1, p1 + inner, mm_tn(nl[16:, cols], gall[:, p1:]))
        store_grads(b, p1 + inner, p1 + 2 * inner, mm_tn(cot[:, cols], glow[...]))
    grads1 = send_grads(1)

    for i in range(nb):
        lo, hi = i * TB, (i + 1) * TB
        g_diag = gmt[lo:hi, lo:hi]
        g_low = jnp.where(below, g_diag, 0.0)
        g_up = jnp.where(above, g_diag, 0.0)
        for pair in range(hl // 2):
            cols = slice(pair * 128, (pair + 1) * 128)
            cols_r = slice(inner + pair * 128, inner + (pair + 1) * 128)
            ds = []
            for h in (2 * pair, 2 * pair + 1):
                fc = cc[lo:hi, h : h + 1]
                rc = cc[lo:hi, hl + h : hl + h + 1]
                fr = cct[h : h + 1, :]
                rr = cct[hl + h : hl + h + 1, :]
                p = jnp.exp(jnp.minimum(fr[:, lo:hi] - fc, rr[:, lo:hi] - rc))
                ups = [(g_up * p).astype(BF16)]
                lows = [(g_low * p).astype(BF16)]
                if i < nb - 1:
                    p = jnp.exp(fr[:, hi:] - fc)
                    ups.append((gmt[lo:hi, hi:] * p).astype(BF16))
                if i > 0:
                    p = jnp.exp(rr[:, :lo] - rc)
                    lows.insert(0, (gmt[lo:hi, :lo] * p).astype(BF16))
                lows = jnp.concatenate(lows, axis=1) if len(lows) > 1 else lows[0]
                ups = jnp.concatenate(ups, axis=1) if len(ups) > 1 else ups[0]
                ds.append((mm(ups, dy[lo:, cols]), mm(lows, dy[:hi, cols])))
            dw[lo:hi, cols] = jnp.where(pair_left, ds[0][0], ds[1][0])
            dw[lo:hi, cols_r] = jnp.where(pair_left, ds[0][1], ds[1][1])

    for i in range(nb):
        lo, hi = i * TB, (i + 1) * TB
        acc_low = jnp.zeros((TB, lo), F32) if i > 0 else None
        acc_up = jnp.zeros((TB, tok - hi), F32) if i < nb - 1 else None
        acc_diag = jnp.zeros((TB, TB), F32)
        for h in range(hl):
            pair = h // 2
            cols = slice(pair * 128, (pair + 1) * 128)
            cols_r = slice(inner + pair * 128, inner + (pair + 1) * 128)
            mine = pair_left if h % 2 == 0 else jnp.logical_not(pair_left)
            d = jnp.where(mine, dy[lo:hi, cols].astype(F32), 0.0).astype(BF16)
            wf = mm_nt(d, w16[:hi, cols])
            wr = mm_nt(d, w16[lo:, cols_r])
            acc_diag = acc_diag + jnp.where(below, wf[:, lo:], wr[:, :TB]) * pexp[h, lo:hi, lo:hi].astype(F32)
            if i > 0:
                acc_low = acc_low + wf[:, :lo] * pexp[h, lo:hi, :lo].astype(F32)
            if i < nb - 1:
                acc_up = acc_up + wr[:, TB:] * pexp[h, lo:hi, hi:].astype(F32)
        parts = ([acc_low] if i > 0 else []) + [acc_diag] + ([acc_up] if i < nb - 1 else [])
        dg[lo:hi, :] = jnp.where(mix_mask(i), jnp.concatenate(parts, axis=1), 0.0).astype(BF16)

    out_ag = gather_chunks(ob, obuf, oag, out_copies)
    onward1 = pass_grads(1, grads1)

    for copy in back_copies:
        copy.wait_recv()
    pending.extend(back_copies)
    acc_f = jnp.zeros((state_n, inner), F32)
    acc_r = jnp.zeros((state_n, inner), F32)
    for k in range(1, nc):
        new = dec_spread[k - 1][:, :inner] * acc_f + dbuf[k - 1].astype(F32)
        acc_f = jnp.where(k > c, new, acc_f)
    for k in range(nc - 1, 0, -1):
        new = dec_spread[k - 1][:, inner:] * acc_r + dbuf[k - 1].astype(F32)
        acc_r = jnp.where(k <= c, new, acc_r)
    back16[:, :inner] = acc_f.astype(BF16)
    back16[:, inner:] = acc_r.astype(BF16)
    dec_own = exact_right(dec[...], spread)[0:1, :]
    last_row = dec_own * jnp.sum(
        back16[...].astype(F32) * into16[...].astype(F32), axis=0, keepdims=True
    )

    for i in range(nb):
        rows = slice(i * TB, (i + 1) * TB)
        bgt = mm(low[rows, inner : inner + state_n], back16[...])
        w = w16[rows, :].astype(F32)
        qb = q16[rows, :].astype(F32) * bgt
        last_row = last_row + jnp.sum(qb, axis=0, keepdims=True)
        dwl = dw[rows, :]
        dwt = dwl + tol[rows, :] * bgt
        x = low[rows, :inner].astype(F32)
        dted = dte[rows, :] * dwt
        gx = dted[:, :inner] + dted[:, inner:] + skip_row * dmix[rows, :]
        du[rows, :inner] = gx.astype(BF16).astype(F32)
        d = dy[rows, :].astype(F32)
        ac = jnp.concatenate([d, d], axis=1) * yfr[rows, :] - w * dwl - qb
        xd = jnp.concatenate([x, x], axis=1) * dwt
        dcc[rows, :] = exact_right(ac, spread, mm_nt)
        ddt[rows, :] = exact_right(xd, spread, mm_nt)
    last_heads = exact_right(jnp.broadcast_to(last_row, (8, 2 * inner)), spread, mm_nt)[0:1, :]
    place = iota((tok, 1), 0)
    at_end = ((place == tok - 1) & is_fwd) | ((place == 0) & jnp.logical_not(is_fwd))
    dc_all = dcc[...] + jnp.where(at_end, last_heads, 0.0)
    dsums = exact_left(tri, dc_all)
    dld = jnp.where(is_fwd, dsums[tok - 1 : tok, :] - dsums + dc_all, dsums)
    gdt = (ddt[...] + dld * rate_row) * jax.nn.sigmoid(dtr[...])
    gall[:, conv_w:p1] = gdt.astype(BF16)
    misc = slice(conv_w, conv_w + 128)
    sm[...] = jnp.zeros(sm.shape, F32)
    sm[0, 5:6, :inner] = acc_gain
    sm[0, 3:4, misc] = exact_right(
        jnp.broadcast_to(acc_skip, (8, inner)), spread[:, :inner], mm_nt
    )[0:1, :]
    sm[0, 1:2, misc] = jnp.sum(gdt, axis=0, keepdims=True)
    sm[0, 2:3, misc] = jnp.sum(dld * ld[...], axis=0, keepdims=True)

    db = mm_tn(dg[...], c16) + mm_nt(q16[...], back16[...])
    dc = mm(dg[...], b16) + mm_nt(rdy[...], into16[...])
    du[0:tok, inner:] = jnp.concatenate([db, dc], axis=1)
    edge = None
    for i in range(nb):
        rows = slice(i * TB, (i + 1) * TB)
        uu = u[rows, :]
        sg = jax.nn.sigmoid(uu)
        du[rows, :] = du[rows, :] * (sg * (1.0 + uu * (1.0 - sg)))
        if edge is None:
            edge = remote(du.at[pl.ds(0, 8)], du.at[pl.ds(tok, 8)], cx(nc - 1))
    edge.wait_recv()
    pending.append(edge)
    conv_acc = [jnp.zeros((1, conv_w), F32) for _ in range(taps)]
    for i in range(nb):
        lo, hi = i * TB, (i + 1) * TB
        here = seg_col(lo, TB)
        x_rows = xp[16 + lo : 16 + hi, :]
        acc = jnp.zeros((TB, conv_w), F32)
        for d in range(taps):
            m = du[lo + d : hi + d, :]
            if d > 0:
                m = m * (seg_col(lo, TB, d) == here).astype(F32)
            acc = acc + m * kc[taps - 1 - d : taps - d, :]
            conv_acc[taps - 1 - d] = conv_acc[taps - 1 - d] + jnp.sum(m * x_rows, axis=0, keepdims=True)
        gall[lo:hi, :conv_w] = acc.astype(BF16)
    for k in range(taps):
        sm[0, 1 + k : 2 + k, :conv_w] = conv_acc[k]

    w_all = weights(0, p1 + inner)
    acc_norm = jnp.zeros((1, width), F32)
    for i in range(tok // 256):
        rows = slice(i * 256, (i + 1) * 256)
        part = mm_nt(gall[rows, :], w_all)
        hb[rows, :] = part.astype(BF16)
        h = hid[rows, :].astype(F32)
        rr = lax.rsqrt(jnp.mean(h * h, axis=1, keepdims=True) + EPS)
        acc_norm = acc_norm + jnp.sum(part * (h * rr), axis=0, keepdims=True)
    sm[0, 0:1, :] = acc_norm
    head_copies = spread_chunks(hb, hpbuf)

    for b in range(width // block):
        cols = slice(b * block, (b + 1) * block)
        store_grads(b, 0, p1, mm_tn(nl[16:, cols], gall[:, :p1]))
    grads0 = send_grads(0)

    slot = 0
    for level, sends in enumerate(
        ([cx(k) for k in range(1, nc)], [fs(k) for k in range(1, nf)], [tx(k) for k in range(1, nt)])
    ):
        copies = [remote(sm.at[level], smbuf.at[slot + k], dev) for k, dev in enumerate(sends)]
        acc = sm[level]
        for k, copy in enumerate(copies):
            copy.wait_recv()
            acc = acc + smbuf[slot + k]
        pending.extend(copies)
        slot += len(sends)
        if level < 2:
            sm[level + 1] = acc
    both = ((iota((8, width), 0) == 0)
            | ((iota((8, width), 1) >= inner) & (iota((8, width), 1) < conv_w)
               & (iota((8, width), 0) >= 1) & (iota((8, width), 0) <= taps)))
    small[...] = jnp.where(both, acc, sm[2])

    onward0 = pass_grads(0, grads0)
    head_ag = gather_chunks(hb, hpbuf, hag, head_copies)

    got = finish_grads(1, onward1)
    gwz[...] = got[:, :inner]
    gwo[...] = got[:, inner:]
    got = finish_grads(0, onward0)
    gwx[...] = got[:, :inner]
    gwdt[...] = got[:, conv_w:]
    bcs[...] = got[:, inner:conv_w].astype(BF16)
    bc_copies = [remote(bcs, bcbuf.at[k - 1], tx(k)) for k in range(1, nt)]
    acc = got[:, inner:conv_w]
    for k in range(1, nt):
        bc_copies[k - 1].wait_recv()
        acc = acc + bcbuf[k - 1].astype(F32)
    pending.extend(bc_copies)
    gwbc[...] = acc

    for copy in out_ag + head_ag:
        copy.wait_recv()
    pending.extend(out_ag + head_ag)

    @pl.loop(0, nb)
    def _(i):
        rows = pl.ds(pl.multiple_of(i * TB, TB), TB)
        h = hid[rows, :].astype(F32)
        out[rows, :] = (h + oag[rows, :].astype(F32)).astype(BF16)
        rr = lax.rsqrt(jnp.mean(h * h, axis=1, keepdims=True) + EPS)
        q = hag[rows, :].astype(F32) * gain_row
        inner_mean = jnp.mean(q * h, axis=1, keepdims=True)
        gh[rows, :] = cot[rows, :].astype(F32) + rr * (q - h * (rr * rr * inner_mean))

    for copy in pending:
        copy.wait_send()


def per_device(dims, hidden, seq_lengths, norm_gain, weight_x, weight_z, weight_bc, weight_dt,
               conv_x, conv_bc, dt_bias, log_rate, skip_scale, gate_gain, weight_out, cotangent):
    nf, nc, nt = dims
    tok, width = hidden.shape
    rows_w, inner = weight_x.shape
    hl = skip_scale.shape[0]
    shards = nf * nc
    p1 = inner + 256
    cw = p1 + 2 * inner
    conv_w = inner + 128
    state_n = weight_bc.shape[1] // 2
    wdt = jnp.pad(weight_dt.reshape(rows_w, 2 * hl), ((0, 0), (0, 128 - 2 * hl)))
    wsh = jnp.concatenate([weight_x, weight_bc, wdt, weight_z, weight_out.T], axis=1)
    kc = jnp.concatenate([conv_x, conv_bc], axis=1)
    hrow = jnp.pad(
        jnp.stack([dt_bias.reshape(-1), log_rate.reshape(-1)]), ((0, 6), (0, 128 - 2 * hl))
    )
    prow = jnp.stack([jnp.repeat(skip_scale, inner // hl), gate_gain])
    chunk = tok // nt
    n_small = nf + nc + nt - 3
    scratch = {
        "hbuf": ((16, width), BF16),
        "nl": ((tok + 16, width), BF16),
        "wbuf": ((shards, rows_w, cw), BF16),
        "xp": ((tok + 16, conv_w), F32),
        "dtr": ((tok, 128), F32),
        "u": ((tok, conv_w), F32),
        "low": ((tok, conv_w), BF16),
        "z": ((tok, inner), F32),
        "ggate": ((tok, inner), BF16),
        "ld": ((tok, 128), F32),
        "cc": ((tok, 128), F32),
        "cct": ((128, tok), F32),
        "dte": ((tok, 2 * inner), F32),
        "rea": ((tok, 2 * inner), F32),
        "tol": ((tok, 2 * inner), F32),
        "w16": ((tok, 2 * inner), BF16),
        "q16": ((tok, 2 * inner), BF16),
        "gm": ((tok, tok), F32),
        "gmt": ((tok, tok), F32),
        "pexp": ((hl, tok, tok), BF16),
        "yfr": ((tok, 2 * inner), F32),
        "s16": ((state_n, 2 * inner), BF16),
        "sbuf": ((nc - 1, state_n, inner), BF16),
        "dec": ((8, 128), F32),
        "decbuf": ((nc - 1, 8, 128), F32),
        "into16": ((state_n, 2 * inner), BF16),
        "gated": ((tok, inner), F32),
        "mixed": ((tok, inner), F32),
        "dmix": ((tok, inner), F32),
        "dy": ((tok, inner), BF16),
        "st": ((8, tok), F32),
        "stbuf": ((nt - 1, 8, tok), F32),
        "gall": ((tok, p1 + inner), BF16),
        "glow": ((tok, inner), BF16),
        "ob": ((tok, width), BF16),
        "obuf": ((nt - 1, chunk, width), BF16),
        "oag": ((tok, width), BF16),
        "hb": ((tok, width), BF16),
        "hpbuf": ((nt - 1, chunk, width), BF16),
        "hag": ((tok, width), BF16),
        "rdy": ((tok, 2 * inner), BF16),
        "d16": ((state_n, 2 * inner), BF16),
        "dbuf": ((nc - 1, state_n, inner), BF16),
        "back16": ((state_n, 2 * inner), BF16),
        "dg": ((tok, tok), BF16),
        "dw": ((tok, 2 * inner), F32),
        "dcc": ((tok, 128), F32),
        "ddt": ((tok, 128), F32),
        "du": ((tok + 8, conv_w), F32),
        "gw16": ((shards, rows_w, cw), BF16),
        "fbuf": ((nf - 1, nc, rows_w, cw), BF16),
        "hsend": ((nc, rows_w, cw), BF16),
        "cbuf": ((nc - 1, rows_w, cw), BF16),
        "bcs": ((rows_w, 128), BF16),
        "bcbuf": ((nt - 1, rows_w, 128), BF16),
        "sm": ((3, 8, width), F32),
        "smbuf": ((n_small, 8, width), F32),
    }
    n_sems = 1 + 2 * (nc + nf - 2 + (nc - 1) * (nf - 1)) + 3 * (nc - 1) + 5 * (nt - 1) + 1
    n_sems += 2 * (nf - 1 + nc - 1) + n_small + nt - 1
    vmem = pl.BlockSpec(memory_space=pltpu.VMEM)
    f32 = lambda *shape: jax.ShapeDtypeStruct(shape, F32)
    out, gh, gwx, gwz, gwbc, gwdt, gwo, small = pl.pallas_call(
        partial(mixer_kernel, (nf, nc, nt, hl)),
        out_shape=(
            jax.ShapeDtypeStruct((tok, width), BF16), f32(tok, width),
            f32(rows_w, inner), f32(rows_w, inner), f32(rows_w, 128), f32(rows_w, 128),
            f32(rows_w, inner), f32(8, width),
        ),
        in_specs=[pl.BlockSpec(memory_space=pltpu.SMEM)] + [vmem] * 7,
        out_specs=[vmem] * 8,
        scratch_shapes=[pltpu.VMEM(s, d) for s, d in scratch.values()]
        + [pltpu.SemaphoreType.DMA((n_sems,)), pltpu.SemaphoreType.DMA((n_sems,))],
        compiler_params=pltpu.CompilerParams(
            collective_id=0, has_side_effects=True, vmem_limit_bytes=60 << 20
        ),
    )(seq_lengths, hidden, norm_gain[None, :], wsh, kc, hrow, prow, cotangent)
    misc = small[:, conv_w : conv_w + 2 * hl]
    return (
        out, gh, small[0], gwx, gwz, gwbc, gwdt[:, : 2 * hl].reshape(rows_w, 2, hl),
        small[1:5, :inner], small[1:5, inner:conv_w],
        misc[1].reshape(2, hl), misc[2].reshape(2, hl), misc[3, :hl],
        small[5, :inner], gwo.T,
    )


def solution(mesh):
    dims = tuple(mesh.shape[a] for a in ("fsdp", "ctx", "tp"))
    both = ("fsdp", "ctx")
    return jax.shard_map(
        partial(per_device, dims),
        mesh=mesh,
        in_specs=(
            P(both, None), P("fsdp", None), P(), P(both, "tp"), P(both, "tp"), P(both, None),
            P(both, None, "tp"), P(None, "tp"), P(), P(None, "tp"), P(None, "tp"), P("tp"),
            P("tp"), P("tp", both), P(both, None),
        ),
        out_specs=(
            P(both, None), P(both, None), P(), P(both, "tp"), P(both, "tp"), P(both, None),
            P(both, None, "tp"), P(None, "tp"), P(), P(None, "tp"), P(None, "tp"), P("tp"),
            P("tp"), P("tp", both),
        ),
        check_vma=False,
    )
```

time: 903 us -> 142 us (0.16); the launches traced: 888 us -> 142 us
  local copies, waits for them, and re-layouts: 278 us -> 25.1 us
  blocking collectives: 226 us -> 0 us
  waiting for transfers between devices: 130 us -> 0 us
  Pallas kernels: 0 us -> 113 us
  other arithmetic: 114 us -> 2.5 us
  matrix products: 103 us -> 0 us
  between operations: 20.8 us -> 0.7 us
  starting transfers between devices: 10.8 us -> 0 us
    all_gather x9 -> x0, blocking collectives: 170 us -> none  [the longest x4 39.2 us: prefix(): lax.all_gather(part.astype(kind), axis)]
    dynamic_update_slice x56 -> x0, local copies, waits for them, and re-layouts: 133 us -> none  [direction_pass(): lax.scan(jax.checkpoint(span_pass), (state_in, seg_prior), pieces)]
    pallas_call x0 -> x1, Pallas kernels: none -> 113 us  [per_device(): pl.pallas_call(partial(mixer_kernel, (nf, nc, nt, hl)), out_shape=(jax.Sh...]
    reduce_scatter x4 -> x0, waiting for transfers between devices: 112 us -> none  [the longest x1 36.3 us: per_device(): lax.psum_scatter(grad_z.astype(jnp.bfloat16), ('fsdp', 'ctx'), scatter_di...]
    dot_general x133 -> x0, matrix products: 103 us -> none  [the longest x24 29.8 us: span_pass(): jnp.einsum('ij,ijh,jhp->ihp', scores, mixing, weighted, precision=highest)]
    psum x3 -> x0, blocking collectives: 48.6 us -> none  [the longest x1 27.9 us: per_device(): lax.psum((grad_norm_gain, grad_conv_x, grad_conv_bc, grad_bias_carry + gr...]
    squeeze x56 -> x1, local copies, waits for them, and re-layouts: 42.7 us -> 1.31 us  [per_device(): misc[3, :hl]]
    convert_element_type x55 -> x0, other arithmetic: 40.5 us -> none  [the longest x16 17.3 us: span_pass(): (seg_block == seg_block[length - 1]).astype(jnp.float32)[:, None]]
  transfers between devices with their start and end apart: 10 -> 0, of which waited for: 6 -> 0; matrix products, arithmetic and copies ran while one was open for 6% -> 0% of each run, Pallas kernels for 0% -> 0%
where the time goes in v1:
time: 142 us
  Pallas kernels  113 us (80%)
  local copies, waits for them, and re-layouts  25.1 us (18%)
  other arithmetic  2.5 us (2%)
    pallas_call x1, Pallas kernels, per_device(): pl.pallas_call(partial(mixer_kernel, (nf, nc, nt, hl)), out_shape=(jax.Sh...  113 us
    unnamed x24, local copies, waits for them, and re-layouts  10.4 us

profile of v1, /device:TPU:0, one launch (start us, length us, event | category | flops | bytes accessed | tf_op | source)
XLA Modules:
  0.0 141.6 jit_solution(2699141149040999309)
XLA Ops:
  0.6 0.8 stack_reshape.9
  1.4 0.8 stack_reshape.10
  2.2 0.7 stack.10
  2.8 0.6 select_maximum_fusion.refs_5_
  3.4 1.3 broadcast_in_dim.6.refs_2_
  4.7 0.7 copy.31
  5.4 0.7 broadcast_in_dim.7
  6.2 0.6 pad_maximum_fusion.1.refs_6_
  6.8 1.3 pad_maximum_fusion.refs_4_
  8.1 0.1 copy.32
  8.2 0.9 constant_dynamic-update-slice_fusion.2
  9.1 0.7 constant_dynamic-update-slice_fusion.1
  9.9 0.9 constant_dynamic-update-slice_fusion
  10.8 0.9 bitcast_dynamic-update-slice_fusion.refs_3_
  11.7 0.7 copy-done.1
  12.4 113.3 %shard_map.254 = (bf16[512,768]{1,0:T(8,128)(2,1)}, f32[512,768]{1,0:T(8,128)}, f32[96,384]{1,0:T(8,128)}, f32[96,384]{1,0:T(8,128)}, f32[96,128]{1,0:T(8,128)},...) custom-call(s32[1,4]{1,0:T(1,128)} %refs_0_.1, bf16[512,768]{1,0:T(8,128)(2,1)} %refs_1_.1, ...), custom_call_target="tpu_custom_call" | custom-call | tf_op jit(solution)/shard_map/pallas_call | solution.py:744
  125.7 1.3 slice_bitcast_fusion
  127.0 0.8 slice_reduce_fusion.2
  127.8 0.6 reshape_squeeze.7
  128.4 0.6 reshape_squeeze.6
  129.1 1.3 slice_reduce_fusion.1
  130.4 1.2 slice.31
  131.6 1.3 slice_reduce_fusion
  133.0 1.3 slice.30
  134.3 0.9 copy.33
  135.1 0.6 copy.34
  135.8 2.1 %copy.45 = bf16[512,768]{1,0:T(8,128)(2,1)} copy(bf16[512,768]{1,0:T(8,128)(2,1)} %get-tuple-element.74) | data formatting | bytes 1572864
  137.8 1.1 copy.46
  139.0 0.7 copy.47
  139.7 0.7 copy.48
  140.3 0.6 copy.49
  140.9 0.7 copy.50
  (15 shorter events, 0.1 us)
Async XLA Ops:
  11.7 0.7 copy-start.1
  125.7 12.1 %copy-start = (f32[512,768]{1,0:T(8,128)S(1)}, f32[512,768]{1,0:T(8,128)}, u32[]{:S(2)}) copy-start(f32[512,768]{1,0:T(8,128)} %get-tuple-element.75) | copy-start | bytes 4718596
  137.8 1.2 copy-start.4
  137.8 1.8 %copy-start.3 = (f32[96,384]{1,0:T(8,128)S(1)}, f32[96,384]{1,0:T(8,128)}, u32[]{:S(2)}) copy-start(f32[96,384]{1,0:T(8,128)} %get-tuple-element.78) | copy-start | bytes 442372
  137.8 2.5 %copy-start.5 = (f32[96,128]{1,0:T(8,128)S(1)}, f32[96,128]{1,0:T(8,128)}, u32[]{:S(2)}) copy-start(f32[96,128]{1,0:T(8,128)} %get-tuple-element.79) | copy-start | bytes 147460
  137.8 3.1 %copy-start.2 = (f32[96,384]{1,0:T(8,128)S(1)}, f32[96,384]{1,0:T(8,128)}, u32[]{:S(2)}) copy-start(f32[96,384]{1,0:T(8,128)} %get-tuple-element.29) | copy-start | bytes 442372

commit v2 on v1

v2 whole, which is shorter than its diff:
```python
from functools import partial

import jax
import jax.numpy as jnp
from jax import lax
from jax.experimental import pallas as pl
from jax.experimental.pallas import tpu as pltpu
from jax.sharding import PartitionSpec as P

MESH = pl.DeviceIdType.MESH
F32 = jnp.float32
BF16 = jnp.bfloat16
EPS = 1e-05
TB = 128
PR = 64
LAG = 3
PUMP = (
    (0, 1, 1, 1), (1, 1, 1, 1), (1, 1, 1, 1), (0, 1, 0, 1), (0, 1, 0, 1), (0, 1, 0, 1), (2, 4, 6, 6, 6)
)


def mm(left, right):
    return lax.dot_general(left, right, (((1,), (0,)), ((), ())), preferred_element_type=F32)


def mm_nt(left, right):
    return lax.dot_general(left, right, (((1,), (1,)), ((), ())), preferred_element_type=F32)


def mm_tn(left, right):
    return lax.dot_general(left, right, (((0,), (0,)), ((), ())), preferred_element_type=F32)


def split3(value):
    high = value.astype(BF16)
    rest = value - high.astype(F32)
    middle = rest.astype(BF16)
    low = (rest - middle.astype(F32)).astype(BF16)
    return high, middle, low


def exact_left(ones, value, dot=mm):
    a, b, c = split3(value)
    return dot(ones, a) + dot(ones, b) + dot(ones, c)


def exact_right(value, ones, dot=mm):
    a, b, c = split3(value)
    return dot(a, ones) + dot(b, ones) + dot(c, ones)


def iota(shape, dim):
    return lax.broadcasted_iota(jnp.int32, shape, dim)


def mixer_kernel(dims, *refs):
    (lens, hid, gain, wx, wz, wbc, wdt, wot, conv_x, conv_bc, dtb, rate, skip, ggain, cot, oag, hag,
     gwx, gwz, gwbc, gwdt, gwo, small, hbuf, nl, wbuf, xp, dtr, u, low, z, ggate, ld, cc, cct, dte,
     rea, tol, w16, q16, gm, gmt, pexp, yfr, s16, sbuf, dec, decbuf, into16, gated, mixed, dmix, dy,
     st, stbuf, gall, glow, ob, oin, oex, hb, hin, hex_, rdy, d16, dbuf, back16, dg, dw, dcc, ddt,
     du, gw16, fbuf, hsend, cbuf, bcs, bcbuf, sm, smbuf, ssem, rsem) = refs
    nf, nc, nt, hl = dims
    tok, width = hid.shape
    rows_w, inner = wx.shape
    pdim = inner // hl
    state_n = wbc.shape[1] // 2
    xo = 2 * state_n
    conv_w = xo + inner
    off = (0, xo + 128, xo + 128 + inner, xo + 128 + 2 * inner, xo + 128 + 3 * inner)
    gall_w = off[3]
    nb = tok // TB
    taps = conv_x.shape[0]
    f, c, t = lax.axis_index("fsdp"), lax.axis_index("ctx"), lax.axis_index("tp")
    base = c * tok
    counter = [0]
    pending = []

    def take(count):
        counter[0] += count
        return counter[0] - count

    def describe(i, src, dst, dev):
        return pltpu.make_async_remote_copy(
            src_ref=src, dst_ref=dst, send_sem=ssem.at[i], recv_sem=rsem.at[i],
            device_id=dev, device_id_type=MESH,
        )

    def remote(src, dst, dev):
        copy = describe(take(1), src, dst, dev)
        copy.start()
        pending.append(copy)
        return copy

    def fs(k):
        return (lax.rem(f + k, nf), c, t)

    def cx(k):
        return (f, lax.rem(c + k, nc), t)

    def tx(k):
        return (f, c, lax.rem(t + k, nt))

    barrier = pltpu.get_barrier_semaphore()
    peers = [fs(k) for k in range(1, nf)] + [cx(k) for k in range(1, nc)] + [tx(k) for k in range(1, nt)]
    for dev in peers:
        pl.semaphore_signal(barrier, inc=1, device_id=dev, device_id_type=MESH)

    me = f * nc + c
    wbuf[me, :, 0:xo] = wbc[...]
    flat = jnp.concatenate(
        [wdt[h].astype(F32) for h in range(hl)] + [jnp.zeros((16 - 2 * hl, rows_w), F32)], axis=0
    ).astype(BF16)
    lane_of = lax.rem(iota((16, 128), 0), 2) * hl + lax.div(iota((16, 128), 0), 2)
    turn = (iota((16, 128), 1) == lane_of).astype(F32).astype(BF16)
    wbuf[me, :, xo : off[1]] = mm_tn(flat, turn).astype(BF16)
    wbuf[me, :, off[1] : off[2]] = wx[...]
    wbuf[me, :, off[2] : off[3]] = wz[...]
    wbuf[me, :, off[3] : off[4]] = wot[...]

    lane = iota((1, 128), 1)
    is_fwd = lane < hl
    bias_row = jnp.zeros((1, 128), F32)
    log_row = jnp.zeros((1, 128), F32)
    for d in range(2):
        for h in range(hl):
            bias_row = jnp.where(lane == d * hl + h, dtb[d, h], bias_row)
            log_row = jnp.where(lane == d * hl + h, rate[d, h], log_row)
    rate_row = -jnp.exp(log_row)
    head_of = lax.div(iota((1, inner), 1), pdim)
    skip_row = jnp.zeros((1, inner), F32)
    for h in range(hl):
        skip_row = jnp.where(head_of == h, skip[h], skip_row)
    gain_row = gain[...].reshape(1, width)
    gain_gate = ggain[...].reshape(1, inner)

    def norm_low(rows):
        h = rows.astype(F32)
        r = lax.rsqrt(jnp.mean(h * h, axis=1, keepdims=True) + EPS)
        return (h * r * gain_row).astype(BF16)

    @pl.loop(0, nb)
    def _(i):
        at = pl.multiple_of(i * TB, TB)
        nl[pl.ds(16 + at, TB), :] = norm_low(hid[pl.ds(at, TB), :])

    pl.semaphore_wait(barrier, len(peers))

    col_parts = [pl.ds(off[p], off[p + 1] - off[p]) for p in range(4)]
    rim = remote(hid.at[pl.ds(tok - 16, 16)], hbuf, cx(1))
    ctx_copies = []
    fwd_copies = []
    for cols in col_parts:
        own = wbuf.at[me, :, cols]
        ctx_copies.append([remote(own, own, cx(k)) for k in range(1, nc)])
        fwd_copies.append([remote(own, own, fs(k)) for k in range(1, nf)])

    def pass_weights(part):
        for k in range(1, nc):
            ctx_copies[part][k - 1].wait_recv()
            src = wbuf.at[f * nc + lax.rem(c + nc - k, nc), :, col_parts[part]]
            for j in range(1, nf):
                fwd_copies[part].append(remote(src, src, fs(j)))

    def get_weights(part):
        for copy in fwd_copies[part]:
            copy.wait_recv()

    def weights(lo, hi):
        if rows_w % 16 == 0:
            return wbuf[:, :, lo:hi].reshape(width, hi - lo)
        return wbuf[:, :, lo:hi].astype(F32).reshape(width, hi - lo).astype(BF16)

    ends = []
    total = lens[0, 0]
    ends.append(total)
    for k in range(1, lens.shape[1]):
        total = total + lens[0, k]
        ends.append(total)

    def seg_of(pos):
        seg = jnp.where(pos < 0, -1, 0)
        for e in ends:
            seg = seg + jnp.where(pos >= e, 1, 0)
        return seg

    one_pos = jnp.full((1, 1), 0, jnp.int32)
    seg_before = seg_of(one_pos + (base - 1))
    seg_first = seg_of(one_pos + base)
    seg_last = seg_of(one_pos + (base + tok - 1))
    seg_after = seg_of(one_pos + (base + tok))
    seg_row = seg_of(iota((1, tok), 1) + base)
    place_row = iota((1, tok), 1)

    def seg_col(start, count, shift=0):
        return seg_of(iota((count, 1), 0) + (base + start + shift))

    spread = (
        iota((128, 2 * inner), 0) == lax.div(iota((128, 2 * inner), 1), pdim)
    ).astype(F32).astype(BF16)
    tri = (iota((tok, tok), 0) >= iota((tok, tok), 1)).astype(F32).astype(BF16)
    seg_all = seg_col(0, tok)

    rim.wait_recv()
    nl[0:16, :] = norm_low(hbuf[...])
    pass_weights(0)
    get_weights(0)

    w_part = weights(off[0], off[1])
    xp[0:16, :xo] = mm(nl[0:16, :], w_part)[:, :xo]
    for i in range(tok // 256):
        got = mm(nl[16 + i * 256 : 16 + (i + 1) * 256, :], w_part)
        xp[16 + i * 256 : 16 + (i + 1) * 256, :xo] = got[:, :xo]
        dtr[i * 256 : (i + 1) * 256, :] = got[:, xo:] + bias_row

    def conv_forward(cols, taps_ref):
        for i in range(nb):
            lo = i * TB
            here = seg_col(lo, TB)
            acc = xp[16 + lo : 16 + lo + TB, cols] * taps_ref[taps - 1 : taps, :]
            for d in range(1, taps):
                match = (seg_col(lo, TB, -d) == here).astype(F32)
                acc = acc + xp[16 + lo - d : 16 + lo - d + TB, cols] * taps_ref[taps - 1 - d : taps - d, :] * match
            u[lo : lo + TB, cols] = acc
            low[lo : lo + TB, cols] = (acc * jax.nn.sigmoid(acc)).astype(BF16)

    bc_cols, x_cols = slice(0, xo), slice(xo, conv_w)
    conv_forward(bc_cols, conv_bc)
    raw = dtr[...]
    step = jnp.maximum(raw, 0.0) + jnp.log1p(jnp.exp(-jnp.abs(raw)))
    decay = step * rate_row
    ld[...] = decay
    sums = exact_left(tri, decay)
    tot = sums[tok - 1 : tok, :]
    cum = jnp.where(is_fwd, sums, tot - sums + decay)
    cc[...] = cum
    cct[...] = cum.T
    dec_mask = jnp.where(
        is_fwd,
        (seg_last == seg_before).astype(F32),
        (seg_first == seg_after).astype(F32),
    )
    dec[...] = jnp.broadcast_to(jnp.exp(tot) * dec_mask, (8, 128))
    dec_copies = [remote(dec, decbuf.at[k - 1], cx(k)) for k in range(1, nc)]
    reach = jnp.exp(cum) * jnp.where(
        is_fwd, (seg_all == seg_before).astype(F32), (seg_all == seg_after).astype(F32)
    )
    to_end = jnp.exp(tot - cum) * jnp.where(
        is_fwd, (seg_all == seg_last).astype(F32), (seg_all == seg_first).astype(F32)
    )
    dte[...] = exact_right(step, spread)
    tol[...] = exact_right(to_end, spread)
    pass_weights(1)
    rea[...] = exact_right(reach, spread)

    b16 = low[:, 0:state_n]
    c16 = low[:, state_n:xo]

    def mix_mask(i):
        same = seg_col(i * TB, TB) == seg_row
        return same & (iota((TB, 1), 0) + i * TB != place_row)

    for i in range(nb):
        lo, hi = i * TB, (i + 1) * TB
        mask = mix_mask(i)
        gm[lo:hi, :] = jnp.where(mask, mm_nt(c16[lo:hi], b16), 0.0)
        gmt[lo:hi, :] = jnp.where(mask, mm_nt(b16[lo:hi], c16), 0.0)

    get_weights(1)
    w_part = weights(off[1], off[2])
    xp[0:16, xo:] = mm(nl[0:16, :], w_part)
    for i in range(tok // 256):
        xp[16 + i * 256 : 16 + (i + 1) * 256, xo:] = mm(nl[16 + i * 256 : 16 + (i + 1) * 256, :], w_part)
    conv_forward(x_cols, conv_x)

    @pl.loop(0, nb)
    def _(i):
        rows = pl.ds(pl.multiple_of(i * TB, TB), TB)
        x = low[rows, xo:].astype(F32)
        w = (jnp.concatenate([x, x], axis=1) * dte[rows, :]).astype(BF16)
        w16[rows, :] = w
        q16[rows, :] = (w.astype(F32) * tol[rows, :]).astype(BF16)

    s16[...] = mm_tn(b16, q16[...]).astype(BF16)

    def half_of(forward):
        return pl.ds(pl.multiple_of(jnp.where(forward, 0, inner), 128), inner)

    state_copies = []
    for k in range(1, nc):
        forward = lax.rem(c + k, nc) > c
        state_copies.append(remote(s16.at[:, half_of(forward)], sbuf.at[k - 1], cx(k)))

    local = iota((TB, TB), 0)
    below = local > iota((TB, TB), 1)
    above = local < iota((TB, TB), 1)
    pair_left = iota((1, 128), 1) < pdim

    def pair_cols(pair):
        return (
            slice(pair * 128, (pair + 1) * 128),
            slice(inner + pair * 128, inner + (pair + 1) * 128),
        )

    def beside(parts):
        return jnp.concatenate(parts, axis=1) if len(parts) > 1 else parts[0]

    for i in range(nb):
        lo, hi = i * TB, (i + 1) * TB
        if i == 2:
            pass_weights(2)
        g_diag = gm[lo:hi, lo:hi]
        g_low = jnp.where(below, g_diag, 0.0)
        g_up = jnp.where(above, g_diag, 0.0)
        for pair in range(hl // 2):
            cols, cols_r = pair_cols(pair)
            ys = []
            for h in (2 * pair, 2 * pair + 1):
                fc = cc[lo:hi, h : h + 1]
                rc = cc[lo:hi, hl + h : hl + h + 1]
                fr = cct[h : h + 1, :]
                rr = cct[hl + h : hl + h + 1, :]
                p = jnp.exp(jnp.minimum(fc - fr[:, lo:hi], rc - rr[:, lo:hi]))
                pexp[h, lo:hi, lo:hi] = p.astype(BF16)
                lows = [(g_low * p).astype(BF16)]
                ups = [(g_up * p).astype(BF16)]
                if i > 0:
                    p = jnp.exp(fc - fr[:, :lo])
                    pexp[h, lo:hi, :lo] = p.astype(BF16)
                    lows.insert(0, (gm[lo:hi, :lo] * p).astype(BF16))
                if i < nb - 1:
                    p = jnp.exp(rc - rr[:, hi:])
                    pexp[h, lo:hi, hi:] = p.astype(BF16)
                    ups.append((gm[lo:hi, hi:] * p).astype(BF16))
                ys.append((mm(beside(lows), w16[:hi, cols]), mm(beside(ups), w16[lo:, cols_r])))
            yfr[lo:hi, cols] = jnp.where(pair_left, ys[0][0], ys[1][0])
            yfr[lo:hi, cols_r] = jnp.where(pair_left, ys[0][1], ys[1][1])

    get_weights(2)
    w_part = weights(off[2], off[3])
    for i in range(tok // 256):
        z[i * 256 : (i + 1) * 256, :] = mm(nl[16 + i * 256 : 16 + (i + 1) * 256, :], w_part)
    pass_weights(3)
    get_weights(3)
    wo = weights(off[3], off[4])
    for i in range(tok // 256):
        rows = slice(i * 256, (i + 1) * 256)
        ggate[rows, :] = mm(cot[rows, :], wo).astype(BF16)

    dec_spread = []
    for k in range(1, nc):
        dec_copies[k - 1].wait_recv()
        dec_spread.append(exact_right(decbuf[k - 1], spread)[0:1, :])
    for copy in state_copies:
        copy.wait_recv()
    acc_f = jnp.zeros((state_n, inner), F32)
    acc_r = jnp.zeros((state_n, inner), F32)
    for k in range(nc - 1, 0, -1):
        new = dec_spread[k - 1][:, :inner] * acc_f + sbuf[k - 1].astype(F32)
        acc_f = jnp.where(k <= c, new, acc_f)
    for k in range(1, nc):
        new = dec_spread[k - 1][:, inner:] * acc_r + sbuf[k - 1].astype(F32)
        acc_r = jnp.where(k > c, new, acc_r)
    into16[:, :inner] = acc_f.astype(BF16)
    into16[:, inner:] = acc_r.astype(BF16)

    row_s = (iota((8, inner), 0) == 0).astype(F32).astype(BF16)
    row_t = (iota((8, inner), 0) == 1).astype(F32).astype(BF16)
    for i in range(nb):
        rows = slice(i * TB, (i + 1) * TB)
        carried = mm(low[rows, state_n:xo], into16[...]) * rea[rows, :]
        y = yfr[rows, :] + carried
        yfr[rows, :] = y
        mix = y[:, :inner] + y[:, inner:] + skip_row * low[rows, xo:].astype(F32)
        mixed[rows, :] = mix
        zz = z[rows, :]
        gt = mix * zz * jax.nn.sigmoid(zz)
        gated[rows, :] = gt
        s = exact_left(row_s, gt * gt, mm_nt)
        s = s + exact_left(row_t, ggate[rows, :].astype(F32) * gain_gate * gt, mm_nt)
        st[:, rows] = s
    st_copies = [remote(st, stbuf.at[k - 1], tx(k)) for k in range(1, nt)]
    rows_sum = st[...]
    for k in range(1, nt):
        st_copies[k - 1].wait_recv()
    for k in range(nt):
        part = jnp.where(t == k, st[...], 0.0)
        for j in range(1, nt):
            part = jnp.where(lax.rem(t + nt - j, nt) == k, stbuf[j - 1], part)
        rows_sum = part if k == 0 else rows_sum + part
    total_inner = inner * nt
    r_row = lax.rsqrt(rows_sum[0:1, :] * (1.0 / total_inner) + EPS)
    q_row = r_row * r_row * r_row * rows_sum[1:2, :] * (-1.0 / total_inner)
    row8 = iota((8, tok), 0)
    rq = jnp.where(row8 == 0, r_row, jnp.where(row8 == 1, q_row, 0.0))
    pick = (iota((8, 256), 0) == lax.div(iota((8, 256), 1), 128)).astype(F32).astype(BF16)
    rq_cols = exact_right(rq, pick, mm_tn)

    is_mid = (t > 0) & (t < nt - 1)
    is_end = (t == 0) | (t == nt - 1)
    inside = (f, c, 1 + lax.div(t, nt - 1))
    across = (f, c, nt - 1 - t)
    outside = (f, c, (t - 1) * (nt - 1))
    pieces = tok // PR

    def piece(ref, p):
        return ref.at[pl.ds(p * PR, PR)]

    class Line:
        def __init__(self, own, inbox, exchange, sums):
            self.own, self.inbox, self.exchange, self.sums = own, inbox, exchange, sums
            self.ids = take(3 * pieces)

        def up(self, p):
            return describe(self.ids + p, piece(self.own, p), self.inbox.at[p], inside)

        def over(self, p):
            return describe(self.ids + pieces + p, piece(self.own, p), self.exchange.at[p], across)

        def down(self, p):
            return describe(self.ids + 2 * pieces + p, piece(self.sums, p), piece(self.sums, p), outside)

        def first(self, p):
            self.up(p).wait_recv()
            rows = slice(p * PR, (p + 1) * PR)
            both = self.own[rows, :].astype(F32) + self.inbox[p].astype(F32)
            self.own[rows, :] = both.astype(BF16)
            self.over(p).start()

        def second(self, p):
            self.over(p).wait_recv()
            rows = slice(p * PR, (p + 1) * PR)
            both = self.own[rows, :].astype(F32) + self.exchange[p].astype(F32)
            self.sums[rows, :] = both.astype(BF16)
            self.down(p).start()

        def begin(self, p_list):
            @pl.when(is_end)
            def _():
                for p in p_list:
                    self.up(p).start()

        def close(self):
            @pl.when(is_end)
            def _():
                for p in range(pieces):
                    self.down(p).wait_recv()
                for p in range(pieces):
                    self.up(p).wait_send()

            @pl.when(is_mid)
            def _():
                for p in range(pieces):
                    self.over(p).wait_send()
                    self.down(p).wait_send()

        def actions(self):
            todo = []
            for p in range(pieces + LAG):
                if p < pieces:
                    todo.append(partial(self.first, p))
                if p >= LAG:
                    todo.append(partial(self.second, p - LAG))
            return todo

    line_o = Line(ob, oin, oex, oag)
    line_h = Line(hb, hin, hex_, hag)
    todo = line_o.actions()

    def pump(count):
        now = [todo.pop(0) for _ in range(min(count, len(todo)))]
        if now:
            @pl.when(is_mid)
            def _():
                for action in now:
                    action()

    acc_gain = jnp.zeros((1, inner), F32)
    acc_skip = jnp.zeros((1, inner), F32)
    for i in range(nb):
        rows = slice(i * TB, (i + 1) * TB)
        r = rq_cols[rows, 0:1]
        q = rq_cols[rows, 128:129]
        gt = gated[rows, :]
        gg = ggate[rows, :].astype(F32)
        ghat = gt * r
        gl = (ghat * gain_gate).astype(BF16)
        glow[rows, :] = gl
        ob[rows, :] = mm_nt(gl, wo).astype(BF16)
        line_o.begin(range(i * TB // PR, (i + 1) * TB // PR))
        acc_gain = acc_gain + jnp.sum(gg * ghat, axis=0, keepdims=True)
        ggated = gg * gain_gate * r + gt * q
        zz = z[rows, :]
        sg = jax.nn.sigmoid(zz)
        dm = ggated * zz * sg
        mix = mixed[rows, :]
        gall[rows, off[2] :] = (ggated * mix * (sg * (1.0 + zz * (1.0 - sg)))).astype(BF16)
        dmix[rows, :] = dm
        acc_skip = acc_skip + jnp.sum(dm * low[rows, xo:].astype(F32), axis=0, keepdims=True)
        d = dm.astype(BF16)
        dy[rows, :] = d
        rdy[rows, :] = (jnp.concatenate([d, d], axis=1).astype(F32) * rea[rows, :]).astype(BF16)

    d16[...] = mm_tn(low[:, state_n:xo], rdy[...]).astype(BF16)
    back_copies = []
    for k in range(1, nc):
        forward = lax.rem(c + k, nc) < c
        back_copies.append(remote(d16.at[:, half_of(forward)], dbuf.at[k - 1], cx(k)))

    col_sets = ((0, off[2]), (off[2], off[4]))

    def send_grads(part):
        lo, hi = col_sets[part]
        copies = []
        for k in range(1, nf):
            to = pl.ds(lax.rem(f + k, nf) * nc, nc)
            copies.append(
                remote(gw16.at[to, :, pl.ds(lo, hi - lo)], fbuf.at[k - 1, :, :, pl.ds(lo, hi - lo)], fs(k))
            )
        return copies

    def pass_grads(part, copies):
        lo, hi = col_sets[part]
        for copy in copies:
            copy.wait_recv()
        onward = []
        for k in list(range(1, nc)) + [0]:
            to = lax.rem(c + k, nc)
            acc = gw16[f * nc + to, :, lo:hi].astype(F32)
            for j in range(1, nf):
                acc = acc + fbuf[j - 1, to, :, lo:hi].astype(F32)
            hsend[k, :, lo:hi] = acc.astype(BF16)
            if k > 0:
                onward.append(
                    remote(hsend.at[k, :, pl.ds(lo, hi - lo)], cbuf.at[k - 1, :, pl.ds(lo, hi - lo)], cx(k))
                )
        return onward

    def finish_grads(part, onward):
        lo, hi = col_sets[part]
        for copy in onward:
            copy.wait_recv()
        acc = hsend[0, :, lo:hi].astype(F32)
        for k in range(1, nc):
            acc = acc + cbuf[k - 1, :, lo:hi].astype(F32)
        return acc

    block = 384
    per = block // rows_w

    def store_grads(b, lo, hi, value):
        for s in range(per):
            gw16[b * per + s, :, lo:hi] = value[s * rows_w : (s + 1) * rows_w].astype(BF16)

    for b in range(width // block):
        cols = slice(b * block, (b + 1) * block)
        store_grads(b, off[2], off[3], mm_tn(nl[16:, cols], gall[:, off[2] :]))
        store_grads(b, off[3], off[4], mm_tn(cot[:, cols], glow[...]))
    grads1 = send_grads(1)

    for i in range(nb):
        lo, hi = i * TB, (i + 1) * TB
        g_diag = gmt[lo:hi, lo:hi]
        g_low = jnp.where(below, g_diag, 0.0)
        g_up = jnp.where(above, g_diag, 0.0)
        for pair in range(hl // 2):
            cols, cols_r = pair_cols(pair)
            ds = []
            for h in (2 * pair, 2 * pair + 1):
                fc = cc[lo:hi, h : h + 1]
                rc = cc[lo:hi, hl + h : hl + h + 1]
                fr = cct[h : h + 1, :]
                rr = cct[hl + h : hl + h + 1, :]
                p = jnp.exp(jnp.minimum(fr[:, lo:hi] - fc, rr[:, lo:hi] - rc))
                ups = [(g_up * p).astype(BF16)]
                lows = [(g_low * p).astype(BF16)]
                if i < nb - 1:
                    p = jnp.exp(fr[:, hi:] - fc)
                    ups.append((gmt[lo:hi, hi:] * p).astype(BF16))
                if i > 0:
                    p = jnp.exp(rr[:, :lo] - rc)
                    lows.insert(0, (gmt[lo:hi, :lo] * p).astype(BF16))
                ds.append((mm(beside(ups), dy[lo:, cols]), mm(beside(lows), dy[:hi, cols])))
            dw[lo:hi, cols] = jnp.where(pair_left, ds[0][0], ds[1][0])
            dw[lo:hi, cols_r] = jnp.where(pair_left, ds[0][1], ds[1][1])
        pump(PUMP[0][i])

    for i in range(nb):
        lo, hi = i * TB, (i + 1) * TB
        acc_low = jnp.zeros((TB, lo), F32) if i > 0 else None
        acc_up = jnp.zeros((TB, tok - hi), F32) if i < nb - 1 else None
        acc_diag = jnp.zeros((TB, TB), F32)
        for h in range(hl):
            cols, cols_r = pair_cols(h // 2)
            mine = pair_left if h % 2 == 0 else jnp.logical_not(pair_left)
            d = jnp.where(mine, dy[lo:hi, cols].astype(F32), 0.0).astype(BF16)
            wf = mm_nt(d, w16[:hi, cols])
            wr = mm_nt(d, w16[lo:, cols_r])
            acc_diag = acc_diag + jnp.where(below, wf[:, lo:], wr[:, :TB]) * pexp[h, lo:hi, lo:hi].astype(F32)
            if i > 0:
                acc_low = acc_low + wf[:, :lo] * pexp[h, lo:hi, :lo].astype(F32)
            if i < nb - 1:
                acc_up = acc_up + wr[:, TB:] * pexp[h, lo:hi, hi:].astype(F32)
        parts = ([acc_low] if i > 0 else []) + [acc_diag] + ([acc_up] if i < nb - 1 else [])
        dg[lo:hi, :] = jnp.where(mix_mask(i), beside(parts), 0.0).astype(BF16)
        pump(PUMP[1][i])

    onward1 = pass_grads(1, grads1)

    for copy in back_copies:
        copy.wait_recv()
    acc_f = jnp.zeros((state_n, inner), F32)
    acc_r = jnp.zeros((state_n, inner), F32)
    for k in range(1, nc):
        new = dec_spread[k - 1][:, :inner] * acc_f + dbuf[k - 1].astype(F32)
        acc_f = jnp.where(k > c, new, acc_f)
    for k in range(nc - 1, 0, -1):
        new = dec_spread[k - 1][:, inner:] * acc_r + dbuf[k - 1].astype(F32)
        acc_r = jnp.where(k <= c, new, acc_r)
    back16[:, :inner] = acc_f.astype(BF16)
    back16[:, inner:] = acc_r.astype(BF16)
    dec_own = exact_right(dec[...], spread)[0:1, :]
    last_row = dec_own * jnp.sum(
        back16[...].astype(F32) * into16[...].astype(F32), axis=0, keepdims=True
    )

    for i in range(nb):
        rows = slice(i * TB, (i + 1) * TB)
        bgt = mm(low[rows, 0:state_n], back16[...])
        w = w16[rows, :].astype(F32)
        qb = q16[rows, :].astype(F32) * bgt
        last_row = last_row + jnp.sum(qb, axis=0, keepdims=True)
        dwl = dw[rows, :]
        dwt = dwl + tol[rows, :] * bgt
        x = low[rows, xo:].astype(F32)
        dted = dte[rows, :] * dwt
        gx = dted[:, :inner] + dted[:, inner:] + skip_row * dmix[rows, :]
        du[rows, xo:] = gx.astype(BF16).astype(F32)
        d = dy[rows, :].astype(F32)
        ac = jnp.concatenate([d, d], axis=1) * yfr[rows, :] - w * dwl - qb
        xd = jnp.concatenate([x, x], axis=1) * dwt
        dcc[rows, :] = exact_right(ac, spread, mm_nt)
        ddt[rows, :] = exact_right(xd, spread, mm_nt)
        pump(PUMP[2][i])
    last_heads = exact_right(jnp.broadcast_to(last_row, (8, 2 * inner)), spread, mm_nt)[0:1, :]
    place = iota((tok, 1), 0)
    at_end = ((place == tok - 1) & is_fwd) | ((place == 0) & jnp.logical_not(is_fwd))
    dc_all = dcc[...] + jnp.where(at_end, last_heads, 0.0)
    dsums = exact_left(tri, dc_all)
    dld = jnp.where(is_fwd, dsums[tok - 1 : tok, :] - dsums + dc_all, dsums)
    gdt = (ddt[...] + dld * rate_row) * jax.nn.sigmoid(dtr[...])
    gall[:, xo : off[1]] = gdt.astype(BF16)
    misc = slice(conv_w, conv_w + 128)
    sm[...] = jnp.zeros(sm.shape, F32)
    sm[0, 5:6, :inner] = acc_gain
    sm[0, 3:4, misc] = exact_right(
        jnp.broadcast_to(acc_skip, (8, inner)), spread[:, :inner], mm_nt
    )[0:1, :]
    sm[0, 1:2, misc] = jnp.sum(gdt, axis=0, keepdims=True)
    sm[0, 2:3, misc] = jnp.sum(dld * ld[...], axis=0, keepdims=True)

    db = mm_tn(dg[...], c16) + mm_nt(q16[...], back16[...])
    dc = mm(dg[...], b16) + mm_nt(rdy[...], into16[...])
    du[0:tok, :xo] = jnp.concatenate([db, dc], axis=1)
    edge = None
    for i in range(nb):
        rows = slice(i * TB, (i + 1) * TB)
        uu = u[rows, :]
        sg = jax.nn.sigmoid(uu)
        du[rows, :] = du[rows, :] * (sg * (1.0 + uu * (1.0 - sg)))
        if edge is None:
            edge = remote(du.at[pl.ds(0, 8)], du.at[pl.ds(tok, 8)], cx(nc - 1))
        pump(PUMP[3][i])
    edge.wait_recv()
    taps_of = jnp.concatenate([conv_bc[...], conv_x[...]], axis=1)
    conv_acc = [jnp.zeros((1, conv_w), F32) for _ in range(taps)]
    for i in range(nb):
        lo, hi = i * TB, (i + 1) * TB
        here = seg_col(lo, TB)
        x_rows = xp[16 + lo : 16 + hi, :]
        acc = jnp.zeros((TB, conv_w), F32)
        for d in range(taps):
            m = du[lo + d : hi + d, :]
            if d > 0:
                m = m * (seg_col(lo, TB, d) == here).astype(F32)
            acc = acc + m * taps_of[taps - 1 - d : taps - d, :]
            conv_acc[taps - 1 - d] = conv_acc[taps - 1 - d] + jnp.sum(m * x_rows, axis=0, keepdims=True)
        gall[lo:hi, :xo] = acc[:, :xo].astype(BF16)
        gall[lo:hi, off[1] : off[2]] = acc[:, xo:].astype(BF16)
        pump(PUMP[4][i])
    for k in range(taps):
        sm[0, 1 + k : 2 + k, :conv_w] = conv_acc[k]

    w_all = weights(0, gall_w)
    acc_norm = jnp.zeros((1, width), F32)
    for i in range(nb):
        rows = slice(i * TB, (i + 1) * TB)
        part = mm_nt(gall[rows, :], w_all)
        hb[rows, :] = part.astype(BF16)
        line_h.begin(range(i * TB // PR, (i + 1) * TB // PR))
        h = hid[rows, :].astype(F32)
        rr = lax.rsqrt(jnp.mean(h * h, axis=1, keepdims=True) + EPS)
        acc_norm = acc_norm + jnp.sum(part * (h * rr), axis=0, keepdims=True)
        pump(PUMP[5][i])
    sm[0, 0:1, :] = acc_norm
    late = line_h.actions()
    mixed_todo = []
    while todo or late:
        if todo:
            mixed_todo.append(todo.pop(0))
        if late:
            mixed_todo.append(late.pop(0))
    todo.extend(mixed_todo)

    def small_send(level, slot, sends):
        return [remote(sm.at[level], smbuf.at[slot + k], dev) for k, dev in enumerate(sends)]

    def small_sum(level, slot, copies):
        acc = sm[level]
        for k, copy in enumerate(copies):
            copy.wait_recv()
            acc = acc + smbuf[slot + k]
        return acc

    sm0 = small_send(0, 0, [cx(k) for k in range(1, nc)])

    for b in range(width // block):
        cols = slice(b * block, (b + 1) * block)
        got = mm_tn(nl[16:, cols], gall[:, : off[2]])
        store_grads(b, 0, off[2], got)
    grads0 = send_grads(0)
    pump(PUMP[6][0])
    sm[1] = small_sum(0, 0, sm0)
    sm1 = small_send(1, nc - 1, [fs(k) for k in range(1, nf)])
    onward0 = pass_grads(0, grads0)
    pump(PUMP[6][1])
    sm[2] = small_sum(1, nc - 1, sm1)
    sm2 = small_send(2, nc + nf - 2, [tx(k) for k in range(1, nt)])
    got = finish_grads(1, onward1)
    gwz[...] = got[:, :inner]
    gwo[...] = got[:, inner:]
    pump(PUMP[6][2])
    got = finish_grads(0, onward0)
    gwx[...] = got[:, off[1] :]
    gwdt[...] = got[:, xo : off[1]]
    bcs[...] = got[:, :xo].astype(BF16)
    bc_copies = [remote(bcs, bcbuf.at[k - 1], tx(k)) for k in range(1, nt)]
    pump(PUMP[6][3])
    shape8 = (8, width)
    over_tp = (iota(shape8, 0) == 0) | (
        (iota(shape8, 1) < xo) & (iota(shape8, 0) >= 1) & (iota(shape8, 0) <= taps)
    )
    acc = sm[2]
    for copy in sm2:
        copy.wait_recv()

    def tp_order(own, box, first):
        total = None
        for k in range(nt):
            part = jnp.where(t == k, own, 0.0)
            for j in range(1, nt):
                part = jnp.where(lax.rem(t + nt - j, nt) == k, box[first + j - 1].astype(F32), part)
            total = part if total is None else total + part
        return total

    small[...] = jnp.where(over_tp, tp_order(sm[2], smbuf, nc + nf - 2), acc)
    pump(PUMP[6][4])
    for copy in bc_copies:
        copy.wait_recv()
    gwbc[...] = tp_order(bcs[...].astype(F32), bcbuf, 0)
    pump(len(todo))

    line_o.close()
    line_h.close()
    for copy in pending:
        copy.wait_send()


def finish_kernel(dims, hid, cot, gain, hsum, osum, gx, gz, gbc, gdt, go, small,
                  out, gh, o_norm, o_x, o_z, o_bc, o_dt, o_cx, o_cbc, o_bias, o_rate, o_skip, o_gain, o_out):
    hl, xo = dims
    width = hid.shape[1]
    rows_w, inner = gx.shape
    h = hid[...].astype(F32)
    out[...] = (h + osum[...].astype(F32)).astype(BF16)
    rr = lax.rsqrt(jnp.mean(h * h, axis=1, keepdims=True) + EPS)
    q = hsum[...].astype(F32) * gain[...].reshape(1, width)
    inner_mean = jnp.mean(q * h, axis=1, keepdims=True)
    gh[...] = cot[...].astype(F32) + rr * (q - h * (rr * rr * inner_mean))

    @pl.when(pl.program_id(0) == 0)
    def _():
        conv_w = xo + inner
        o_norm[...] = small[0:1, :].reshape(width)
        o_x[...] = gx[...]
        o_z[...] = gz[...]
        o_bc[...] = gbc[...]
        o_out[...] = go[...]
        flat = jnp.concatenate([gdt[...], jnp.zeros((128 - rows_w, 128), F32)], axis=0).T
        for k in range(hl):
            for d in range(2):
                o_dt[k, d : d + 1, :] = flat[d * hl + k : d * hl + k + 1, :rows_w]
        taps = o_cx.shape[0]
        o_cx[...] = small[1 : 1 + taps, xo:conv_w]
        o_cbc[...] = small[1 : 1 + taps, :xo]
        for row, ref in ((1, o_bias), (2, o_rate)):
            for d in range(2):
                ref[d : d + 1, :] = small[row : row + 1, conv_w + d * hl : conv_w + (d + 1) * hl]
        o_skip[...] = small[3:4, conv_w : conv_w + hl].reshape(hl)
        o_gain[...] = small[5:6, :inner].reshape(inner)


def per_device(dims, hidden, seq_lengths, norm_gain, weight_x, weight_z, weight_bc, weight_dt,
               conv_x, conv_bc, dt_bias, log_rate, skip_scale, gate_gain, weight_out, cotangent):
    nf, nc, nt = dims
    tok, width = hidden.shape
    rows_w, inner = weight_x.shape
    hl = skip_scale.shape[0]
    shards = nf * nc
    xo = weight_bc.shape[1]
    state_n = xo // 2
    taps = conv_x.shape[0]
    conv_w = xo + inner
    p2 = xo + 128 + inner
    cw = p2 + 2 * inner
    pieces = tok // PR
    n_small = nf + nc + nt - 3
    scratch = {
        "hbuf": ((16, width), BF16),
        "nl": ((tok + 16, width), BF16),
        "wbuf": ((shards, rows_w, cw), BF16),
        "xp": ((tok + 16, conv_w), F32),
        "dtr": ((tok, 128), F32),
        "u": ((tok, conv_w), F32),
        "low": ((tok, conv_w), BF16),
        "z": ((tok, inner), F32),
        "ggate": ((tok, inner), BF16),
        "ld": ((tok, 128), F32),
        "cc": ((tok, 128), F32),
        "cct": ((128, tok), F32),
        "dte": ((tok, 2 * inner), F32),
        "rea": ((tok, 2 * inner), F32),
        "tol": ((tok, 2 * inner), F32),
        "w16": ((tok, 2 * inner), BF16),
        "q16": ((tok, 2 * inner), BF16),
        "gm": ((tok, tok), F32),
        "gmt": ((tok, tok), F32),
        "pexp": ((hl, tok, tok), BF16),
        "yfr": ((tok, 2 * inner), F32),
        "s16": ((state_n, 2 * inner), BF16),
        "sbuf": ((nc - 1, state_n, inner), BF16),
        "dec": ((8, 128), F32),
        "decbuf": ((nc - 1, 8, 128), F32),
        "into16": ((state_n, 2 * inner), BF16),
        "gated": ((tok, inner), F32),
        "mixed": ((tok, inner), F32),
        "dmix": ((tok, inner), F32),
        "dy": ((tok, inner), BF16),
        "st": ((8, tok), F32),
        "stbuf": ((nt - 1, 8, tok), F32),
        "gall": ((tok, p2 + inner), BF16),
        "glow": ((tok, inner), BF16),
        "ob": ((tok, width), BF16),
        "oin": ((pieces, PR, width), BF16),
        "oex": ((pieces, PR, width), BF16),
        "hb": ((tok, width), BF16),
        "hin": ((pieces, PR, width), BF16),
        "hex": ((pieces, PR, width), BF16),
        "rdy": ((tok, 2 * inner), BF16),
        "d16": ((state_n, 2 * inner), BF16),
        "dbuf": ((nc - 1, state_n, inner), BF16),
        "back16": ((state_n, 2 * inner), BF16),
        "dg": ((tok, tok), BF16),
        "dw": ((tok, 2 * inner), F32),
        "dcc": ((tok, 128), F32),
        "ddt": ((tok, 128), F32),
        "du": ((tok + 8, conv_w), F32),
        "gw16": ((shards, rows_w, cw), BF16),
        "fbuf": ((nf - 1, nc, rows_w, cw), BF16),
        "hsend": ((nc, rows_w, cw), BF16),
        "cbuf": ((nc - 1, rows_w, cw), BF16),
        "bcs": ((rows_w, xo), BF16),
        "bcbuf": ((nt - 1, rows_w, xo), BF16),
        "sm": ((3, 8, width), F32),
        "smbuf": ((n_small, 8, width), F32),
    }
    n_sems = 2 + 4 * (nc + nf - 2 + (nc - 1) * (nf - 1)) + 3 * (nc - 1) + 2 * (nt - 1)
    n_sems += 2 * (nf - 1 + nc - 1) + n_small + 6 * pieces
    vmem = pl.BlockSpec(memory_space=pltpu.VMEM)
    smem = pl.BlockSpec(memory_space=pltpu.SMEM)
    f32 = lambda *shape: jax.ShapeDtypeStruct(shape, F32)
    bf16 = lambda *shape: jax.ShapeDtypeStruct(shape, BF16)
    osum, hsum, gx, gz, gbc, gdt, go, small = pl.pallas_call(
        partial(mixer_kernel, (nf, nc, nt, hl)),
        out_shape=(
            bf16(tok, width), bf16(tok, width), f32(rows_w, inner), f32(rows_w, inner),
            f32(rows_w, xo), f32(rows_w, 128), f32(rows_w, inner), f32(8, width),
        ),
        in_specs=[smem] + [vmem] * 9 + [smem] * 3 + [vmem] * 2,
        out_specs=[vmem] * 8,
        scratch_shapes=[pltpu.VMEM(s, d) for s, d in scratch.values()]
        + [pltpu.SemaphoreType.DMA((n_sems,)), pltpu.SemaphoreType.DMA((n_sems,))],
        compiler_params=pltpu.CompilerParams(
            collective_id=0, has_side_effects=True, vmem_limit_bytes=60 << 20
        ),
    )(
        seq_lengths, hidden, norm_gain, weight_x, weight_z, weight_bc,
        jnp.transpose(weight_dt, (2, 1, 0)), weight_out.T, conv_x, conv_bc, dt_bias, log_rate,
        skip_scale, gate_gain, cotangent,
    )
    row_block = pl.BlockSpec((TB, width), lambda i: (i, 0))

    def whole(*shape):
        return pl.BlockSpec(shape, lambda i: (0,) * len(shape))

    got = pl.pallas_call(
        partial(finish_kernel, (hl, xo)),
        grid=(tok // TB,),
        out_shape=(
            bf16(tok, width), f32(tok, width), f32(width), f32(rows_w, inner), f32(rows_w, inner),
            f32(rows_w, xo), f32(hl, 2, rows_w), f32(taps, inner), f32(taps, xo), f32(2, hl), f32(2, hl),
            f32(hl), f32(inner), f32(rows_w, inner),
        ),
        in_specs=[
            row_block, row_block, whole(width), row_block, row_block, whole(rows_w, inner),
            whole(rows_w, inner), whole(rows_w, xo), whole(rows_w, 128), whole(rows_w, inner),
            whole(8, width),
        ],
        out_specs=[
            row_block, row_block, whole(width), whole(rows_w, inner), whole(rows_w, inner),
            whole(rows_w, xo), whole(hl, 2, rows_w), whole(taps, inner), whole(taps, xo), whole(2, hl),
            whole(2, hl), whole(hl), whole(inner), whole(rows_w, inner),
        ],
        compiler_params=pltpu.CompilerParams(vmem_limit_bytes=60 << 20),
    )(hidden, cotangent, norm_gain, hsum, osum, gx, gz, gbc, gdt, go, small)
    got = list(got)
    got[6] = jnp.transpose(got[6], (2, 1, 0))
    got[13] = got[13].T
    return tuple(got)


def solution(mesh):
    dims = tuple(mesh.shape[a] for a in ("fsdp", "ctx", "tp"))
    both = ("fsdp", "ctx")
    return jax.shard_map(
        partial(per_device, dims),
        mesh=mesh,
        in_specs=(
            P(both, None), P("fsdp", None), P(), P(both, "tp"), P(both, "tp"), P(both, None),
            P(both, None, "tp"), P(None, "tp"), P(), P(None, "tp"), P(None, "tp"), P("tp"),
            P("tp"), P("tp", both), P(both, None),
        ),
        out_specs=(
            P(both, None), P(both, None), P(), P(both, "tp"), P(both, "tp"), P(both, None),
            P(both, None, "tp"), P(None, "tp"), P(), P(None, "tp"), P(None, "tp"), P("tp"),
            P("tp"), P("tp", both),
        ),
        check_vma=False,
    )
```

time: 142 us -> 95.9 us (0.68)
  local copies, waits for them, and re-layouts: 25.1 us -> 0 us
  Pallas kernels: 113 us -> 94.9 us
  other arithmetic: 2.5 us -> 0 us
    pallas_call x1 -> x2, Pallas kernels: 113 us -> 94.9 us  [the longest x1 89.8 us: per_device(): pl.pallas_call(partial(mixer_kernel, (nf, nc, nt, hl)), out_shape=(bf16(t...]
    unnamed x24 -> x0, local copies, waits for them, and re-layouts: 10.4 us -> none
    slice x6 -> x0, local copies, waits for them, and re-layouts: 6.83 us -> none  [the longest x1 1.34 us: per_device(): small[0]]
    another operation x6 -> x0, local copies, waits for them, and re-layouts: 3.57 us -> none  [the longest x2 1.52 us: per_device(): jnp.stack([dt_bias.reshape(-1), log_rate.reshape(-1)])]
    broadcast_in_dim x2 -> x0, local copies, waits for them, and re-layouts: 1.99 us -> none  [the longest x1 1.27 us: per_device(): norm_gain[None, :]]
where the time goes in v2:
time: 95.9 us; the launch traced here: 95.7 us
  Pallas kernels  94.9 us (99%)
    pallas_call x1, Pallas kernels, per_device(): pl.pallas_call(partial(mixer_kernel, (nf, nc, nt, hl)), out_shape=(bf16(t...  89.8 us
    pallas_call x1, Pallas kernels, per_device(): pl.pallas_call(partial(finish_kernel, (hl, xo)), grid=(tok // TB,), out_s...  5.02 us

profile of v2, /device:TPU:0, one launch (start us, length us, event | category | flops | bytes accessed | tf_op | source)
XLA Modules:
  0.0 95.7 jit_solution(6534154704674851)
XLA Ops:
  0.6 89.8 %shard_map.254 = (bf16[512,768]{1,0:T(8,128)(2,1)}, bf16[512,768]{1,0:T(8,128)(2,1)}, f32[96,384]{1,0:T(8,128)}, f32[96,384]{1,0:T(8,128)}, f32[96,128]{1,0:T(8,...) custom-call(s32[1,4]{1,0:T(1,128)} %refs_0_.1, bf16[512,768]{1,0:T(8,128)(2,1)} %hid.1, f32[768]{0:T(1024)} %gain.1, ...), custom_call_target="tpu_custom_call" | custom-call | tf_op jit(solution)/shard_map/pallas_call | solution.py:892
  90.5 5.0 %shard_map.255 = (bf16[512,768]{1,0:T(8,128)(2,1)}, f32[512,768]{1,0:T(8,128)}, f32[768]{0:T(1024)}, f32[96,384]{1,0:T(8,128)}, f32[96,384]{1,0:T(8,128)}, /*ind...) custom-call(bf16[512,768]{1,0:T(8,128)(2,1)} %hid.1, ...), custom_call_target="tpu_custom_call" | custom-call | tf_op jit(solution)/shard_map/pallas_call | solution.py:915

commit v3 on v2

--- a/solution.py
+++ b/solution.py
@@ -13,9 +13,9 @@
 EPS = 1e-05
 TB = 128
 PR = 64
-LAG = 3
+LAG = 2
 PUMP = (
-    (0, 1, 1, 1), (1, 1, 1, 1), (1, 1, 1, 1), (0, 1, 0, 1), (0, 1, 0, 1), (0, 1, 0, 1), (2, 4, 6, 6, 6)
+    (1, 0, 0, 1), (0, 0, 0, 1), (0, 1, 0, 2), (0, 0, 0, 0), (0, 0, 0, 1), (0, 0, 0, 2), (4, 0, 4, 6, 0, 4, 2)
 )
 
 
@@ -53,17 +53,24 @@
     return lax.broadcasted_iota(jnp.int32, shape, dim)
 
 
+def near_right(value, ones):
+    high = value.astype(BF16)
+    low = (value - high.astype(F32)).astype(BF16)
+    return mm_nt(high, ones) + mm_nt(low, ones)
+
+
 def mixer_kernel(dims, *refs):
-    (lens, hid, gain, wx, wz, wbc, wdt, wot, conv_x, conv_bc, dtb, rate, skip, ggain, cot, oag, hag,
-     gwx, gwz, gwbc, gwdt, gwo, small, hbuf, nl, wbuf, xp, dtr, u, low, z, ggate, ld, cc, cct, dte,
+    (lens, gain, wdt, conv_x, conv_bc, dtb, rate, skip, ggain, hid_h, cot_h, wx_h, wz_h, wbc_h, wot_h,
+     out_h, gh_h, gwx_h, gwz_h, gwbc_h, gwdt_h, gwo_h, small_h,
+     hid, cot, oag, hag, out_v, gh_v, gwx, gwz, gwbc, gwdt, gwo, small, hbuf, nl, wbuf, xp, dtr, u, low, z, zd, ggate, ld, cc, cct, dte,
      rea, tol, w16, q16, gm, gmt, pexp, yfr, s16, sbuf, dec, decbuf, into16, gated, mixed, dmix, dy,
      st, stbuf, gall, glow, ob, oin, oex, hb, hin, hex_, rdy, d16, dbuf, back16, dg, dw, dcc, ddt,
-     du, gw16, fbuf, hsend, cbuf, bcs, bcbuf, sm, smbuf, ssem, rsem) = refs
+     du, gw16, fbuf, hsend, cbuf, bcs, bcbuf, sm, smbuf, tps, tpbuf, ssem, rsem, lsem) = refs
     nf, nc, nt, hl = dims
     tok, width = hid.shape
-    rows_w, inner = wx.shape
+    rows_w, inner = wx_h.shape
     pdim = inner // hl
-    state_n = wbc.shape[1] // 2
+    state_n = wbc_h.shape[1] // 2
     xo = 2 * state_n
     conv_w = xo + inner
     off = (0, xo + 128, xo + 128 + inner, xo + 128 + 2 * inner, xo + 128 + 3 * inner)
@@ -105,17 +112,32 @@
     for dev in peers:
         pl.semaphore_signal(barrier, inc=1, device_id=dev, device_id_type=MESH)
 
+    local_count = [0]
+    local_copies = []
+
+    def bring(src, dst):
+        i = local_count[0]
+        local_count[0] += 1
+        copy = pltpu.make_async_copy(src, dst, lsem.at[i])
+        copy.start()
+        return copy
+
+    def keep(src, dst):
+        local_copies.append(bring(src, dst))
+
     me = f * nc + c
-    wbuf[me, :, 0:xo] = wbc[...]
+    get_hid = bring(hid_h, hid)
+    shard_copies = []
+    for p, src in ((0, wbc_h), (1, wx_h), (2, wz_h), (3, wot_h)):
+        width_p = xo if p == 0 else inner
+        shard_copies.append(bring(src, wbuf.at[me, :, pl.ds(off[p], width_p)]))
+    get_cot = bring(cot_h, cot)
     flat = jnp.concatenate(
         [wdt[h].astype(F32) for h in range(hl)] + [jnp.zeros((16 - 2 * hl, rows_w), F32)], axis=0
     ).astype(BF16)
     lane_of = lax.rem(iota((16, 128), 0), 2) * hl + lax.div(iota((16, 128), 0), 2)
     turn = (iota((16, 128), 1) == lane_of).astype(F32).astype(BF16)
     wbuf[me, :, xo : off[1]] = mm_tn(flat, turn).astype(BF16)
-    wbuf[me, :, off[1] : off[2]] = wx[...]
-    wbuf[me, :, off[2] : off[3]] = wz[...]
-    wbuf[me, :, off[3] : off[4]] = wot[...]
 
     lane = iota((1, 128), 1)
     is_fwd = lane < hl
@@ -138,21 +160,29 @@
         r = lax.rsqrt(jnp.mean(h * h, axis=1, keepdims=True) + EPS)
         return (h * r * gain_row).astype(BF16)
 
+    get_hid.wait()
+
     @pl.loop(0, nb)
     def _(i):
         at = pl.multiple_of(i * TB, TB)
         nl[pl.ds(16 + at, TB), :] = norm_low(hid[pl.ds(at, TB), :])
 
+    for copy in shard_copies:
+        copy.wait()
     pl.semaphore_wait(barrier, len(peers))
 
     col_parts = [pl.ds(off[p], off[p + 1] - off[p]) for p in range(4)]
     rim = remote(hid.at[pl.ds(tok - 16, 16)], hbuf, cx(1))
     ctx_copies = []
     fwd_copies = []
-    for cols in col_parts:
-        own = wbuf.at[me, :, cols]
+
+    def send_weights(part):
+        own = wbuf.at[me, :, col_parts[part]]
         ctx_copies.append([remote(own, own, cx(k)) for k in range(1, nc)])
         fwd_copies.append([remote(own, own, fs(k)) for k in range(1, nf)])
+
+    for part in range(4):
+        send_weights(part)
 
     def pass_weights(part):
         for k in range(1, nc):
@@ -220,8 +250,9 @@
             for d in range(1, taps):
                 match = (seg_col(lo, TB, -d) == here).astype(F32)
                 acc = acc + xp[16 + lo - d : 16 + lo - d + TB, cols] * taps_ref[taps - 1 - d : taps - d, :] * match
-            u[lo : lo + TB, cols] = acc
-            low[lo : lo + TB, cols] = (acc * jax.nn.sigmoid(acc)).astype(BF16)
+            sg = jax.nn.sigmoid(acc)
+            u[lo : lo + TB, cols] = sg * (1.0 + acc * (1.0 - sg))
+            low[lo : lo + TB, cols] = (acc * sg).astype(BF16)
 
     bc_cols, x_cols = slice(0, xo), slice(xo, conv_w)
     conv_forward(bc_cols, conv_bc)
@@ -239,7 +270,7 @@
         (seg_last == seg_before).astype(F32),
         (seg_first == seg_after).astype(F32),
     )
-    dec[...] = jnp.broadcast_to(jnp.exp(tot) * dec_mask, (8, 128))
+    dec[...] = jnp.exp(tot) * dec_mask
     dec_copies = [remote(dec, decbuf.at[k - 1], cx(k)) for k in range(1, nc)]
     reach = jnp.exp(cum) * jnp.where(
         is_fwd, (seg_all == seg_before).astype(F32), (seg_all == seg_after).astype(F32)
@@ -247,10 +278,10 @@
     to_end = jnp.exp(tot - cum) * jnp.where(
         is_fwd, (seg_all == seg_last).astype(F32), (seg_all == seg_first).astype(F32)
     )
-    dte[...] = exact_right(step, spread)
-    tol[...] = exact_right(to_end, spread)
+    dte[...] = mm(step.astype(BF16), spread).astype(BF16)
+    tol[...] = mm(to_end.astype(BF16), spread).astype(BF16)
     pass_weights(1)
-    rea[...] = exact_right(reach, spread)
+    rea[...] = mm(reach.astype(BF16), spread).astype(BF16)
 
     b16 = low[:, 0:state_n]
     c16 = low[:, state_n:xo]
@@ -276,9 +307,9 @@
     def _(i):
         rows = pl.ds(pl.multiple_of(i * TB, TB), TB)
         x = low[rows, xo:].astype(F32)
-        w = (jnp.concatenate([x, x], axis=1) * dte[rows, :]).astype(BF16)
+        w = (jnp.concatenate([x, x], axis=1) * dte[rows, :].astype(F32)).astype(BF16)
         w16[rows, :] = w
-        q16[rows, :] = (w.astype(F32) * tol[rows, :]).astype(BF16)
+        q16[rows, :] = (w.astype(F32) * tol[rows, :].astype(F32)).astype(BF16)
 
     s16[...] = mm_tn(b16, q16[...]).astype(BF16)
 
@@ -338,18 +369,15 @@
     get_weights(2)
     w_part = weights(off[2], off[3])
     for i in range(tok // 256):
-        z[i * 256 : (i + 1) * 256, :] = mm(nl[16 + i * 256 : 16 + (i + 1) * 256, :], w_part)
-    pass_weights(3)
-    get_weights(3)
-    wo = weights(off[3], off[4])
-    for i in range(tok // 256):
-        rows = slice(i * 256, (i + 1) * 256)
-        ggate[rows, :] = mm(cot[rows, :], wo).astype(BF16)
+        zz = mm(nl[16 + i * 256 : 16 + (i + 1) * 256, :], w_part)
+        sg = jax.nn.sigmoid(zz)
+        z[i * 256 : (i + 1) * 256, :] = zz * sg
+        zd[i * 256 : (i + 1) * 256, :] = sg * (1.0 + zz * (1.0 - sg))
 
     dec_spread = []
     for k in range(1, nc):
         dec_copies[k - 1].wait_recv()
-        dec_spread.append(exact_right(decbuf[k - 1], spread)[0:1, :])
+        dec_spread.append(exact_right(jnp.broadcast_to(decbuf[k - 1], (8, 128)), spread)[0:1, :])
     for copy in state_copies:
         copy.wait_recv()
     acc_f = jnp.zeros((state_n, inner), F32)
@@ -363,37 +391,41 @@
     into16[:, :inner] = acc_f.astype(BF16)
     into16[:, inner:] = acc_r.astype(BF16)
 
-    row_s = (iota((8, inner), 0) == 0).astype(F32).astype(BF16)
-    row_t = (iota((8, inner), 0) == 1).astype(F32).astype(BF16)
+    ones8 = jnp.ones((8, inner), BF16)
     for i in range(nb):
         rows = slice(i * TB, (i + 1) * TB)
-        carried = mm(low[rows, state_n:xo], into16[...]) * rea[rows, :]
+        carried = mm(low[rows, state_n:xo], into16[...]) * rea[rows, :].astype(F32)
         y = yfr[rows, :] + carried
         yfr[rows, :] = y
         mix = y[:, :inner] + y[:, inner:] + skip_row * low[rows, xo:].astype(F32)
         mixed[rows, :] = mix
-        zz = z[rows, :]
-        gt = mix * zz * jax.nn.sigmoid(zz)
+        gt = mix * z[rows, :]
         gated[rows, :] = gt
-        s = exact_left(row_s, gt * gt, mm_nt)
-        s = s + exact_left(row_t, ggate[rows, :].astype(F32) * gain_gate * gt, mm_nt)
-        st[:, rows] = s
-    st_copies = [remote(st, stbuf.at[k - 1], tx(k)) for k in range(1, nt)]
-    rows_sum = st[...]
-    for k in range(1, nt):
-        st_copies[k - 1].wait_recv()
-    for k in range(nt):
-        part = jnp.where(t == k, st[...], 0.0)
-        for j in range(1, nt):
-            part = jnp.where(lax.rem(t + nt - j, nt) == k, stbuf[j - 1], part)
-        rows_sum = part if k == 0 else rows_sum + part
+        st[0, :, rows] = mm_nt(ones8, (gt * gt).astype(BF16))[0:1]
+    s_copies = [remote(st.at[0], stbuf.at[0, k - 1], tx(k)) for k in range(1, nt)]
+
+    pass_weights(3)
+    get_weights(3)
+    get_cot.wait()
+    wo = weights(off[3], off[4])
+    for i in range(nb):
+        rows = slice(i * TB, (i + 1) * TB)
+        gg = mm(cot[rows, :], wo).astype(BF16)
+        ggate[rows, :] = gg
+        st[1, :, rows] = mm_nt(ones8, (gg.astype(F32) * gain_gate * gated[rows, :]).astype(BF16))[0:1]
+    t_copies = [remote(st.at[1], stbuf.at[1, k - 1], tx(k)) for k in range(1, nt)]
     total_inner = inner * nt
-    r_row = lax.rsqrt(rows_sum[0:1, :] * (1.0 / total_inner) + EPS)
-    q_row = r_row * r_row * r_row * rows_sum[1:2, :] * (-1.0 / total_inner)
-    row8 = iota((8, tok), 0)
-    rq = jnp.where(row8 == 0, r_row, jnp.where(row8 == 1, q_row, 0.0))
-    pick = (iota((8, 256), 0) == lax.div(iota((8, 256), 1), 128)).astype(F32).astype(BF16)
-    rq_cols = exact_right(rq, pick, mm_tn)
+    pick = (iota((8, 128), 0) == 0).astype(F32).astype(BF16)
+
+    def row_total(which, copies):
+        total = st[which]
+        for k in range(1, nt):
+            copies[k - 1].wait_recv()
+            total = total + stbuf[which, k - 1]
+        return total
+
+    r_row = lax.rsqrt(row_total(0, s_copies) * (1.0 / total_inner) + EPS)
+    r_cols = exact_right(jnp.broadcast_to(r_row, (8, tok)), pick, mm_tn)
 
     is_mid = (t > 0) & (t < nt - 1)
     is_end = (t == 0) | (t == nt - 1)
@@ -406,8 +438,9 @@
         return ref.at[pl.ds(p * PR, PR)]
 
     class Line:
-        def __init__(self, own, inbox, exchange, sums):
+        def __init__(self, own, inbox, exchange, sums, done):
             self.own, self.inbox, self.exchange, self.sums = own, inbox, exchange, sums
+            self.done = done
             self.ids = take(3 * pieces)
 
         def up(self, p):
@@ -429,9 +462,15 @@
         def second(self, p):
             self.over(p).wait_recv()
             rows = slice(p * PR, (p + 1) * PR)
-            both = self.own[rows, :].astype(F32) + self.exchange[p].astype(F32)
-            self.sums[rows, :] = both.astype(BF16)
+            both = (self.own[rows, :].astype(F32) + self.exchange[p].astype(F32)).astype(BF16)
+            self.sums[rows, :] = both
             self.down(p).start()
+            self.done(p, rows, both)
+
+        def last(self, p):
+            self.down(p).wait_recv()
+            rows = slice(p * PR, (p + 1) * PR)
+            self.done(p, rows, self.sums[rows, :])
 
         def begin(self, p_list):
             @pl.when(is_end)
@@ -443,8 +482,6 @@
             @pl.when(is_end)
             def _():
                 for p in range(pieces):
-                    self.down(p).wait_recv()
-                for p in range(pieces):
                     self.up(p).wait_send()
 
             @pl.when(is_mid)
@@ -453,18 +490,32 @@
                     self.over(p).wait_send()
                     self.down(p).wait_send()
 
-        def actions(self):
-            todo = []
-            for p in range(pieces + LAG):
-                if p < pieces:
-                    todo.append(partial(self.first, p))
-                if p >= LAG:
-                    todo.append(partial(self.second, p - LAG))
-            return todo
-
-    line_o = Line(ob, oin, oex, oag)
-    line_h = Line(hb, hin, hex_, hag)
-    todo = line_o.actions()
+    def result(i, src, dst, rows):
+        return pltpu.make_async_copy(src.at[rows], dst.at[rows], lsem.at[i])
+
+    result_ids = local_count[0]
+    local_count[0] += 2 * pieces
+
+    def out_done(p, rows, both):
+        out_v[rows, :] = (hid[rows, :].astype(F32) + both.astype(F32)).astype(BF16)
+        result(result_ids + p, out_v, out_h, pl.ds(p * PR, PR)).start()
+
+    def head_done(p, rows, both):
+        h = hid[rows, :].astype(F32)
+        rr = lax.rsqrt(jnp.mean(h * h, axis=1, keepdims=True) + EPS)
+        q = both.astype(F32) * gain_row
+        inner_mean = jnp.mean(q * h, axis=1, keepdims=True)
+        gh_v[rows, :] = cot[rows, :].astype(F32) + rr * (q - h * (rr * rr * inner_mean))
+        result(result_ids + pieces + p, gh_v, gh_h, pl.ds(p * PR, PR)).start()
+
+    line_o = Line(ob, oin, oex, oag, out_done)
+    line_h = Line(hb, hin, hex_, hag, head_done)
+    todo = []
+    for p in range(2 * pieces + LAG):
+        for q, stage in ((p, 0), (p - LAG, 1)):
+            if 0 <= q < 2 * pieces:
+                line = line_o if q < pieces else line_h
+                todo.append(partial(line.first if stage == 0 else line.second, q % pieces))
 
     def pump(count):
         now = [todo.pop(0) for _ in range(min(count, len(todo)))]
@@ -474,31 +525,42 @@
                 for action in now:
                     action()
 
+    for i in range(nb):
+        rows = slice(i * TB, (i + 1) * TB)
+        gl = (gated[rows, :] * r_cols[rows, 0:1] * gain_gate).astype(BF16)
+        glow[rows, :] = gl
+        ob[rows, :] = mm_nt(gl, wo).astype(BF16)
+        line_o.begin(range(i * TB // PR, (i + 1) * TB // PR))
+
+    block = 384
+    per = block // rows_w
+
+    def store_grads(b, lo, hi, value):
+        for s in range(per):
+            gw16[b * per + s, :, lo:hi] = value[s * rows_w : (s + 1) * rows_w].astype(BF16)
+
+    for b in range(width // block):
+        cols = slice(b * block, (b + 1) * block)
+        store_grads(b, off[3], off[4], mm_tn(cot[:, cols], glow[...]))
+
+    q_row = r_row * r_row * r_row * row_total(1, t_copies) * (-1.0 / total_inner)
+    q_cols = exact_right(jnp.broadcast_to(q_row, (8, tok)), pick, mm_tn)
     acc_gain = jnp.zeros((1, inner), F32)
     acc_skip = jnp.zeros((1, inner), F32)
     for i in range(nb):
         rows = slice(i * TB, (i + 1) * TB)
-        r = rq_cols[rows, 0:1]
-        q = rq_cols[rows, 128:129]
+        r = r_cols[rows, 0:1]
         gt = gated[rows, :]
         gg = ggate[rows, :].astype(F32)
-        ghat = gt * r
-        gl = (ghat * gain_gate).astype(BF16)
-        glow[rows, :] = gl
-        ob[rows, :] = mm_nt(gl, wo).astype(BF16)
-        line_o.begin(range(i * TB // PR, (i + 1) * TB // PR))
-        acc_gain = acc_gain + jnp.sum(gg * ghat, axis=0, keepdims=True)
-        ggated = gg * gain_gate * r + gt * q
-        zz = z[rows, :]
-        sg = jax.nn.sigmoid(zz)
-        dm = ggated * zz * sg
-        mix = mixed[rows, :]
-        gall[rows, off[2] :] = (ggated * mix * (sg * (1.0 + zz * (1.0 - sg)))).astype(BF16)
+        acc_gain = acc_gain + jnp.sum(gg * gt * r, axis=0, keepdims=True)
+        ggated = gg * gain_gate * r + gt * q_cols[rows, 0:1]
+        dm = ggated * z[rows, :]
+        gall[rows, off[2] :] = (ggated * mixed[rows, :] * zd[rows, :]).astype(BF16)
         dmix[rows, :] = dm
         acc_skip = acc_skip + jnp.sum(dm * low[rows, xo:].astype(F32), axis=0, keepdims=True)
         d = dm.astype(BF16)
         dy[rows, :] = d
-        rdy[rows, :] = (jnp.concatenate([d, d], axis=1).astype(F32) * rea[rows, :]).astype(BF16)
+        rdy[rows, :] = (jnp.concatenate([d, d], axis=1).astype(F32) * rea[rows, :].astype(F32)).astype(BF16)
 
     d16[...] = mm_tn(low[:, state_n:xo], rdy[...]).astype(BF16)
     back_copies = []
@@ -544,17 +606,9 @@
             acc = acc + cbuf[k - 1, :, lo:hi].astype(F32)
         return acc
 
-    block = 384
-    per = block // rows_w
-
-    def store_grads(b, lo, hi, value):
-        for s in range(per):
-            gw16[b * per + s, :, lo:hi] = value[s * rows_w : (s + 1) * rows_w].astype(BF16)
-
     for b in range(width // block):
         cols = slice(b * block, (b + 1) * block)
         store_grads(b, off[2], off[3], mm_tn(nl[16:, cols], gall[:, off[2] :]))
-        store_grads(b, off[3], off[4], mm_tn(cot[:, cols], glow[...]))
     grads1 = send_grads(1)
 
     for i in range(nb):
@@ -604,8 +658,6 @@
         dg[lo:hi, :] = jnp.where(mix_mask(i), beside(parts), 0.0).astype(BF16)
         pump(PUMP[1][i])
 
-    onward1 = pass_grads(1, grads1)
-
     for copy in back_copies:
         copy.wait_recv()
     acc_f = jnp.zeros((state_n, inner), F32)
@@ -618,11 +670,15 @@
         acc_r = jnp.where(k <= c, new, acc_r)
     back16[:, :inner] = acc_f.astype(BF16)
     back16[:, inner:] = acc_r.astype(BF16)
-    dec_own = exact_right(dec[...], spread)[0:1, :]
+    dec_own = exact_right(jnp.broadcast_to(dec[...], (8, 128)), spread)[0:1, :]
     last_row = dec_own * jnp.sum(
         back16[...].astype(F32) * into16[...].astype(F32), axis=0, keepdims=True
     )
 
+    db = mm_tn(dg[...], c16) + mm_nt(q16[...], back16[...])
+    dc = mm(dg[...], b16) + mm_nt(rdy[...], into16[...])
+    du[0:tok, :xo] = jnp.concatenate([db, dc], axis=1) * u[:, :xo]
+    edge = None
     for i in range(nb):
         rows = slice(i * TB, (i + 1) * TB)
         bgt = mm(low[rows, 0:state_n], back16[...])
@@ -630,16 +686,18 @@
         qb = q16[rows, :].astype(F32) * bgt
         last_row = last_row + jnp.sum(qb, axis=0, keepdims=True)
         dwl = dw[rows, :]
-        dwt = dwl + tol[rows, :] * bgt
+        dwt = dwl + tol[rows, :].astype(F32) * bgt
         x = low[rows, xo:].astype(F32)
-        dted = dte[rows, :] * dwt
+        dted = dte[rows, :].astype(F32) * dwt
         gx = dted[:, :inner] + dted[:, inner:] + skip_row * dmix[rows, :]
-        du[rows, xo:] = gx.astype(BF16).astype(F32)
+        du[rows, xo:] = gx.astype(BF16).astype(F32) * u[rows, xo:]
+        if edge is None:
+            edge = remote(du.at[pl.ds(0, 8)], du.at[pl.ds(tok, 8)], cx(nc - 1))
         d = dy[rows, :].astype(F32)
         ac = jnp.concatenate([d, d], axis=1) * yfr[rows, :] - w * dwl - qb
         xd = jnp.concatenate([x, x], axis=1) * dwt
-        dcc[rows, :] = exact_right(ac, spread, mm_nt)
-        ddt[rows, :] = exact_right(xd, spread, mm_nt)
+        dcc[rows, :] = near_right(ac, spread)
+        ddt[rows, :] = near_right(xd, spread)
         pump(PUMP[2][i])
     last_heads = exact_right(jnp.broadcast_to(last_row, (8, 2 * inner)), spread, mm_nt)[0:1, :]
     place = iota((tok, 1), 0)
@@ -658,23 +716,14 @@
     sm[0, 1:2, misc] = jnp.sum(gdt, axis=0, keepdims=True)
     sm[0, 2:3, misc] = jnp.sum(dld * ld[...], axis=0, keepdims=True)
 
-    db = mm_tn(dg[...], c16) + mm_nt(q16[...], back16[...])
-    dc = mm(dg[...], b16) + mm_nt(rdy[...], into16[...])
-    du[0:tok, :xo] = jnp.concatenate([db, dc], axis=1)
-    edge = None
-    for i in range(nb):
-        rows = slice(i * TB, (i + 1) * TB)
-        uu = u[rows, :]
-        sg = jax.nn.sigmoid(uu)
-        du[rows, :] = du[rows, :] * (sg * (1.0 + uu * (1.0 - sg)))
-        if edge is None:
-            edge = remote(du.at[pl.ds(0, 8)], du.at[pl.ds(tok, 8)], cx(nc - 1))
-        pump(PUMP[3][i])
-    edge.wait_recv()
+    onward1 = pass_grads(1, grads1)
+
     taps_of = jnp.concatenate([conv_bc[...], conv_x[...]], axis=1)
     conv_acc = [jnp.zeros((1, conv_w), F32) for _ in range(taps)]
     for i in range(nb):
         lo, hi = i * TB, (i + 1) * TB
+        if i == nb - 1:
+            edge.wait_recv()
         here = seg_col(lo, TB)
         x_rows = xp[16 + lo : 16 + hi, :]
         acc = jnp.zeros((TB, conv_w), F32)
@@ -702,14 +751,6 @@
         acc_norm = acc_norm + jnp.sum(part * (h * rr), axis=0, keepdims=True)
         pump(PUMP[5][i])
     sm[0, 0:1, :] = acc_norm
-    late = line_h.actions()
-    mixed_todo = []
-    while todo or late:
-        if todo:
-            mixed_todo.append(todo.pop(0))
-        if late:
-            mixed_todo.append(late.pop(0))
-    todo.extend(mixed_todo)
 
     def small_send(level, slot, sends):
         return [remote(sm.at[level], smbuf.at[slot + k], dev) for k, dev in enumerate(sends)]
@@ -731,28 +772,29 @@
     pump(PUMP[6][0])
     sm[1] = small_sum(0, 0, sm0)
     sm1 = small_send(1, nc - 1, [fs(k) for k in range(1, nf)])
+    pump(PUMP[6][1])
     onward0 = pass_grads(0, grads0)
-    pump(PUMP[6][1])
+    pump(PUMP[6][2])
     sm[2] = small_sum(1, nc - 1, sm1)
-    sm2 = small_send(2, nc + nf - 2, [tx(k) for k in range(1, nt)])
+    parts = [sm[2, 0:1, k * 128 : (k + 1) * 128] for k in range(width // 128)]
+    parts = parts + [sm[2, 1 : 1 + taps, :xo], jnp.zeros((16 - taps - width // 128, 128), F32)]
+    tps[...] = jnp.concatenate(parts, axis=0)
+    tp_copies = [remote(tps, tpbuf.at[k - 1], tx(k)) for k in range(1, nt)]
+    pump(PUMP[6][3])
     got = finish_grads(1, onward1)
     gwz[...] = got[:, :inner]
     gwo[...] = got[:, inner:]
-    pump(PUMP[6][2])
+    keep(gwz, gwz_h)
+    keep(gwo, gwo_h)
+    pump(PUMP[6][4])
     got = finish_grads(0, onward0)
     gwx[...] = got[:, off[1] :]
     gwdt[...] = got[:, xo : off[1]]
+    keep(gwx, gwx_h)
+    keep(gwdt, gwdt_h)
     bcs[...] = got[:, :xo].astype(BF16)
     bc_copies = [remote(bcs, bcbuf.at[k - 1], tx(k)) for k in range(1, nt)]
-    pump(PUMP[6][3])
-    shape8 = (8, width)
-    over_tp = (iota(shape8, 0) == 0) | (
-        (iota(shape8, 1) < xo) & (iota(shape8, 0) >= 1) & (iota(shape8, 0) <= taps)
-    )
-    acc = sm[2]
-    for copy in sm2:
-        copy.wait_recv()
-
+    pump(PUMP[6][5])
     def tp_order(own, box, first):
         total = None
         for k in range(nt):
@@ -762,51 +804,92 @@
             total = part if total is None else total + part
         return total
 
-    small[...] = jnp.where(over_tp, tp_order(sm[2], smbuf, nc + nf - 2), acc)
-    pump(PUMP[6][4])
+    for copy in tp_copies:
+        copy.wait_recv()
+    got = tp_order(tps[...], tpbuf, 0)
+    small[...] = sm[2]
+    for k in range(width // 128):
+        small[0:1, k * 128 : (k + 1) * 128] = got[k : k + 1, :]
+    small[1 : 1 + taps, :xo] = got[width // 128 : width // 128 + taps, :]
+    keep(small, small_h)
+    pump(PUMP[6][6])
     for copy in bc_copies:
         copy.wait_recv()
     gwbc[...] = tp_order(bcs[...].astype(F32), bcbuf, 0)
+    keep(gwbc, gwbc_h)
     pump(len(todo))
+
+    @pl.when(is_end)
+    def _():
+        for line in (line_o, line_h):
+            for p in range(pieces):
+                line.last(p)
 
     line_o.close()
     line_h.close()
+    for p in range(pieces):
+        rows = pl.ds(p * PR, PR)
+        result(result_ids + p, out_v, out_h, rows).wait()
+        result(result_ids + pieces + p, gh_v, gh_h, rows).wait()
+    for copy in local_copies:
+        copy.wait()
     for copy in pending:
         copy.wait_send()
 
 
-def finish_kernel(dims, hid, cot, gain, hsum, osum, gx, gz, gbc, gdt, go, small,
-                  out, gh, o_norm, o_x, o_z, o_bc, o_dt, o_cx, o_cbc, o_bias, o_rate, o_skip, o_gain, o_out):
+def finish_kernel(dims, gdt_h, small_h, gh_h, out_h, gx_h, gz_h, gbc_h, go_h,
+                  gh, out, o_x, o_z, o_bc, o_out, o_norm, o_dt, o_cx, o_cbc, o_bias, o_rate, o_skip, o_gain,
+                  gh_s, out_s, x_s, z_s, bc_s, go_s, norm_s, dt_s, cx_s, cbc_s, bias_s, rate_s, skip_s, gain_s,
+                  gdt, small, sems):
     hl, xo = dims
-    width = hid.shape[1]
-    rows_w, inner = gx.shape
-    h = hid[...].astype(F32)
-    out[...] = (h + osum[...].astype(F32)).astype(BF16)
-    rr = lax.rsqrt(jnp.mean(h * h, axis=1, keepdims=True) + EPS)
-    q = hsum[...].astype(F32) * gain[...].reshape(1, width)
-    inner_mean = jnp.mean(q * h, axis=1, keepdims=True)
-    gh[...] = cot[...].astype(F32) + rr * (q - h * (rr * rr * inner_mean))
-
-    @pl.when(pl.program_id(0) == 0)
-    def _():
-        conv_w = xo + inner
-        o_norm[...] = small[0:1, :].reshape(width)
-        o_x[...] = gx[...]
-        o_z[...] = gz[...]
-        o_bc[...] = gbc[...]
-        o_out[...] = go[...]
-        flat = jnp.concatenate([gdt[...], jnp.zeros((128 - rows_w, 128), F32)], axis=0).T
-        for k in range(hl):
-            for d in range(2):
-                o_dt[k, d : d + 1, :] = flat[d * hl + k : d * hl + k + 1, :rows_w]
-        taps = o_cx.shape[0]
-        o_cx[...] = small[1 : 1 + taps, xo:conv_w]
-        o_cbc[...] = small[1 : 1 + taps, :xo]
-        for row, ref in ((1, o_bias), (2, o_rate)):
-            for d in range(2):
-                ref[d : d + 1, :] = small[row : row + 1, conv_w + d * hl : conv_w + (d + 1) * hl]
-        o_skip[...] = small[3:4, conv_w : conv_w + hl].reshape(hl)
-        o_gain[...] = small[5:6, :inner].reshape(inner)
+    count = [0]
+
+    def move(src, dst):
+        copy = pltpu.make_async_copy(src, dst, sems.at[count[0]])
+        count[0] += 1
+        copy.start()
+        return copy
+
+    first = [move(small_h, small), move(gdt_h, gdt)]
+    moves = []
+    for src, stage, dst, cuts in (
+        (gh_h, gh_s, gh, 4), (out_h, out_s, out, 2), (gx_h, x_s, o_x, 1), (gz_h, z_s, o_z, 1),
+        (go_h, go_s, o_out, 1), (gbc_h, bc_s, o_bc, 1),
+    ):
+        step = src.shape[0] // cuts
+        for k in range(cuts):
+            rows = pl.ds(k * step, step)
+            moves.append((move(src.at[rows], stage.at[rows]), stage.at[rows], dst.at[rows]))
+    rows_w, inner = gx_h.shape
+    width = small.shape[1]
+    conv_w = xo + inner
+    for copy in first:
+        copy.wait()
+    norm_s[...] = small[0:1, :].reshape(width)
+    flat = jnp.concatenate([gdt[...], jnp.zeros((128 - rows_w, 128), F32)], axis=0).T
+    for k in range(hl):
+        for d in range(2):
+            dt_s[k, d : d + 1, :] = flat[d * hl + k : d * hl + k + 1, :rows_w]
+    taps = cx_s.shape[0]
+    cx_s[...] = small[1 : 1 + taps, xo:conv_w]
+    cbc_s[...] = small[1 : 1 + taps, :xo]
+    for row, ref in ((1, bias_s), (2, rate_s)):
+        for d in range(2):
+            ref[d : d + 1, :] = small[row : row + 1, conv_w + d * hl : conv_w + (d + 1) * hl]
+    skip_s[...] = small[3:4, conv_w : conv_w + hl].reshape(hl)
+    gain_s[...] = small[5:6, :inner].reshape(inner)
+    leaving = [
+        move(src, dst)
+        for src, dst in (
+            (norm_s, o_norm), (dt_s, o_dt), (cx_s, o_cx), (cbc_s, o_cbc), (bias_s, o_bias),
+            (rate_s, o_rate), (skip_s, o_skip), (gain_s, o_gain),
+        )
+    ]
+    for into, stage, dst in moves:
+        into.wait()
+        leaving.append(move(stage, dst))
+    for copy in leaving:
+        copy.wait()
 
 
 def per_device(dims, hidden, seq_lengths, norm_gain, weight_x, weight_z, weight_bc, weight_dt,
@@ -823,8 +906,20 @@
     p2 = xo + 128 + inner
     cw = p2 + 2 * inner
     pieces = tok // PR
-    n_small = nf + nc + nt - 3
+    n_small = nf + nc - 2
     scratch = {
+        "hid": ((tok, width), BF16),
+        "cot": ((tok, width), BF16),
+        "oag": ((tok, width), BF16),
+        "hag": ((tok, width), BF16),
+        "out_v": ((tok, width), BF16),
+        "gh_v": ((tok, width), F32),
+        "gwx": ((rows_w, inner), F32),
+        "gwz": ((rows_w, inner), F32),
+        "gwbc": ((rows_w, xo), F32),
+        "gwdt": ((rows_w, 128), F32),
+        "gwo": ((rows_w, inner), F32),
+        "small": ((8, width), F32),
         "hbuf": ((16, width), BF16),
         "nl": ((tok + 16, width), BF16),
         "wbuf": ((shards, rows_w, cw), BF16),
@@ -833,13 +928,14 @@
         "u": ((tok, conv_w), F32),
         "low": ((tok, conv_w), BF16),
         "z": ((tok, inner), F32),
+        "zd": ((tok, inner), F32),
         "ggate": ((tok, inner), BF16),
         "ld": ((tok, 128), F32),
         "cc": ((tok, 128), F32),
         "cct": ((128, tok), F32),
-        "dte": ((tok, 2 * inner), F32),
-        "rea": ((tok, 2 * inner), F32),
-        "tol": ((tok, 2 * inner), F32),
+        "dte": ((tok, 2 * inner), BF16),
+        "rea": ((tok, 2 * inner), BF16),
+        "tol": ((tok, 2 * inner), BF16),
         "w16": ((tok, 2 * inner), BF16),
         "q16": ((tok, 2 * inner), BF16),
         "gm": ((tok, tok), F32),
@@ -848,15 +944,15 @@
         "yfr": ((tok, 2 * inner), F32),
         "s16": ((state_n, 2 * inner), BF16),
         "sbuf": ((nc - 1, state_n, inner), BF16),
-        "dec": ((8, 128), F32),
-        "decbuf": ((nc - 1, 8, 128), F32),
+        "dec": ((1, 128), F32),
+        "decbuf": ((nc - 1, 1, 128), F32),
         "into16": ((state_n, 2 * inner), BF16),
         "gated": ((tok, inner), F32),
         "mixed": ((tok, inner), F32),
         "dmix": ((tok, inner), F32),
         "dy": ((tok, inner), BF16),
-        "st": ((8, tok), F32),
-        "stbuf": ((nt - 1, 8, tok), F32),
+        "st": ((2, 1, tok), F32),
+        "stbuf": ((2, nt - 1, 1, tok), F32),
         "gall": ((tok, p2 + inner), BF16),
         "glow": ((tok, inner), BF16),
         "ob": ((tok, width), BF16),
@@ -882,60 +978,52 @@
         "bcbuf": ((nt - 1, rows_w, xo), BF16),
         "sm": ((3, 8, width), F32),
         "smbuf": ((n_small, 8, width), F32),
+        "tps": ((16, 128), F32),
+        "tpbuf": ((nt - 1, 16, 128), F32),
     }
-    n_sems = 2 + 4 * (nc + nf - 2 + (nc - 1) * (nf - 1)) + 3 * (nc - 1) + 2 * (nt - 1)
-    n_sems += 2 * (nf - 1 + nc - 1) + n_small + 6 * pieces
+    n_sems = 2 + 4 * (nc + nf - 2 + (nc - 1) * (nf - 1)) + 3 * (nc - 1) + 3 * (nt - 1)
+    n_sems += 2 * (nf - 1 + nc - 1) + n_small + 6 * pieces + nt - 1
     vmem = pl.BlockSpec(memory_space=pltpu.VMEM)
     smem = pl.BlockSpec(memory_space=pltpu.SMEM)
     f32 = lambda *shape: jax.ShapeDtypeStruct(shape, F32)
     bf16 = lambda *shape: jax.ShapeDtypeStruct(shape, BF16)
-    osum, hsum, gx, gz, gbc, gdt, go, small = pl.pallas_call(
+    anywhere = pl.BlockSpec(memory_space=pl.ANY)
+    results = pl.pallas_call(
         partial(mixer_kernel, (nf, nc, nt, hl)),
         out_shape=(
-            bf16(tok, width), bf16(tok, width), f32(rows_w, inner), f32(rows_w, inner),
+            bf16(tok, width), f32(tok, width), f32(rows_w, inner), f32(rows_w, inner),
             f32(rows_w, xo), f32(rows_w, 128), f32(rows_w, inner), f32(8, width),
         ),
-        in_specs=[smem] + [vmem] * 9 + [smem] * 3 + [vmem] * 2,
-        out_specs=[vmem] * 8,
+        in_specs=[smem] + [vmem] * 4 + [smem] * 3 + [vmem] + [anywhere] * 6,
+        out_specs=[anywhere] * 8,
         scratch_shapes=[pltpu.VMEM(s, d) for s, d in scratch.values()]
-        + [pltpu.SemaphoreType.DMA((n_sems,)), pltpu.SemaphoreType.DMA((n_sems,))],
+        + [pltpu.SemaphoreType.DMA((n_sems,)), pltpu.SemaphoreType.DMA((n_sems,))]
+        + [pltpu.SemaphoreType.DMA((12 + 2 * pieces,))],
         compiler_params=pltpu.CompilerParams(
-            collective_id=0, has_side_effects=True, vmem_limit_bytes=60 << 20
+            collective_id=0, has_side_effects=True, vmem_limit_bytes=62 << 20
         ),
     )(
-        seq_lengths, hidden, norm_gain, weight_x, weight_z, weight_bc,
-        jnp.transpose(weight_dt, (2, 1, 0)), weight_out.T, conv_x, conv_bc, dt_bias, log_rate,
-        skip_scale, gate_gain, cotangent,
+        seq_lengths, norm_gain, jnp.transpose(weight_dt, (2, 1, 0)), conv_x, conv_bc, dt_bias, log_rate,
+        skip_scale, gate_gain, hidden, cotangent, weight_x, weight_z, weight_bc, weight_out.T,
     )
-    row_block = pl.BlockSpec((TB, width), lambda i: (i, 0))
-
-    def whole(*shape):
-        return pl.BlockSpec(shape, lambda i: (0,) * len(shape))
-
-    got = pl.pallas_call(
+    out, gh, gx, gz, gbc, gdt, go, small = results
+    finals = (
+        f32(tok, width), bf16(tok, width), f32(rows_w, inner), f32(rows_w, inner), f32(rows_w, xo),
+        f32(rows_w, inner), f32(width), f32(hl, 2, rows_w), f32(taps, inner), f32(taps, xo),
+        f32(2, hl), f32(2, hl), f32(hl), f32(inner),
+    )
+    gh, out, gx, gz, gbc, go, norm, gdt, cx, cbc, bias, rate, skip, gate = pl.pallas_call(
         partial(finish_kernel, (hl, xo)),
-        grid=(tok // TB,),
-        out_shape=(
-            bf16(tok, width), f32(tok, width), f32(width), f32(rows_w, inner), f32(rows_w, inner),
-            f32(rows_w, xo), f32(hl, 2, rows_w), f32(taps, inner), f32(taps, xo), f32(2, hl), f32(2, hl),
-            f32(hl), f32(inner), f32(rows_w, inner),
-        ),
-        in_specs=[
-            row_block, row_block, whole(width), row_block, row_block, whole(rows_w, inner),
-            whole(rows_w, inner), whole(rows_w, xo), whole(rows_w, 128), whole(rows_w, inner),
-            whole(8, width),
-        ],
-        out_specs=[
-            row_block, row_block, whole(width), whole(rows_w, inner), whole(rows_w, inner),
-            whole(rows_w, xo), whole(hl, 2, rows_w), whole(taps, inner), whole(taps, xo), whole(2, hl),
-            whole(2, hl), whole(hl), whole(inner), whole(rows_w, inner),
-        ],
-        compiler_params=pltpu.CompilerParams(vmem_limit_bytes=60 << 20),
-    )(hidden, cotangent, norm_gain, hsum, osum, gx, gz, gbc, gdt, go, small)
-    got = list(got)
-    got[6] = jnp.transpose(got[6], (2, 1, 0))
-    got[13] = got[13].T
-    return tuple(got)
+        out_shape=finals,
+        in_specs=[anywhere] * 8,
+        out_specs=[anywhere] * 14,
+        scratch_shapes=[pltpu.VMEM(a.shape, a.dtype) for a in finals]
+        + [pltpu.VMEM((rows_w, 128), F32), pltpu.VMEM((8, width), F32), pltpu.SemaphoreType.DMA((32,))],
+        compiler_params=pltpu.CompilerParams(vmem_limit_bytes=62 << 20),
+    )(gdt, small, gh, out, gx, gz, gbc, go)
+    return (
+        out, gh, norm, gx, gz, gbc, jnp.transpose(gdt, (2, 1, 0)), cx, cbc, bias, rate, skip, gate, go.T
+    )
 
 
 def solution(mesh):

time: 95.9 us -> 85.4 us (0.89)
  Pallas kernels: 94.9 us -> 84.4 us
    pallas_call x1, Pallas kernels: 89.8 us -> 81.5 us  [per_device(): pl.pallas_call(partial(mixer_kernel, (nf, nc, nt, hl)), out_shape=(bf16(t...]
    pallas_call x1, Pallas kernels: 5.02 us -> 2.88 us  [per_device(): pl.pallas_call(partial(finish_kernel, (hl, xo)), out_shape=finals, in_spe...]
where the time goes in v3:
time: 85.4 us; the launch traced here: 85.2 us
  Pallas kernels  84.4 us (99%)
    pallas_call x1, Pallas kernels, per_device(): pl.pallas_call(partial(mixer_kernel, (nf, nc, nt, hl)), out_shape=(bf16(t...  81.5 us
    pallas_call x1, Pallas kernels, per_device(): pl.pallas_call(partial(finish_kernel, (hl, xo)), out_shape=finals, in_spe...  2.88 us

profile of v3, /device:TPU:0, one launch (start us, length us, event | category | flops | bytes accessed | tf_op | source)
XLA Modules:
  0.0 85.2 jit_solution(14121113640114887848)
XLA Ops:
  0.7 81.5 %shard_map.254 = (bf16[512,768]{1,0:T(8,128)(2,1)}, f32[512,768]{1,0:T(8,128)}, f32[96,384]{1,0:T(8,128)}, f32[96,384]{1,0:T(8,128)}, f32[96,128]{1,0:T(8,128)},...) custom-call(s32[1,4]{1,0:T(1,128)} %refs_0_.1, f32[768]{0:T(1024)} %refs_1_.1, bf16[6,2,96]{2,1,0:T(2,128)(2,1)} %bitcast.5, ...), custom_call_target="tpu_custom_call" | custom-call | tf_op jit(solution)/shard_map/pallas_call | solution.py:991
  82.2 2.9 %shard_map.255 = (f32[512,768]{1,0:T(8,128)}, bf16[512,768]{1,0:T(8,128)(2,1)}, f32[96,384]{1,0:T(8,128)}, f32[96,384]{1,0:T(8,128)}, f32[96,128]{1,0:T(8,128)},...) custom-call(f32[96,128]{1,0:T(8,128)} %get-tuple-element.36.gdt_h, ...), custom_call_target="tpu_custom_call" | custom-call | tf_op jit(solution)/shard_map/pallas_call | solution.py:1015

commit v4 on v3

--- a/solution.py
+++ b/solution.py
@@ -15,7 +15,7 @@
 PR = 64
 LAG = 2
 PUMP = (
-    (1, 0, 0, 1), (0, 0, 0, 1), (0, 1, 0, 2), (0, 0, 0, 0), (0, 0, 0, 1), (0, 0, 0, 2), (4, 0, 4, 6, 0, 4, 2)
+    (0, 1, 1, 1), (1, 0, 1, 1), (1, 1, 1, 1), (0, 0, 0, 0), (1, 1, 1, 1), (1, 1, 1, 1), (2, 2, 3, 4, 0, 4, 0)
 )
 
 
@@ -64,7 +64,7 @@
      out_h, gh_h, gwx_h, gwz_h, gwbc_h, gwdt_h, gwo_h, small_h,
      hid, cot, oag, hag, out_v, gh_v, gwx, gwz, gwbc, gwdt, gwo, small, hbuf, nl, wbuf, xp, dtr, u, low, z, zd, ggate, ld, cc, cct, dte,
      rea, tol, w16, q16, gm, gmt, pexp, yfr, s16, sbuf, dec, decbuf, into16, gated, mixed, dmix, dy,
-     st, stbuf, gall, glow, ob, oin, oex, hb, hin, hex_, rdy, d16, dbuf, back16, dg, dw, dcc, ddt,
+     st, stbuf, gall, glow, r_cols, ob, oin, oex, hb, hin, hex_, rdy, d16, dbuf, back16, dg, dw, dcc, ddt,
      du, gw16, fbuf, hsend, cbuf, bcs, bcbuf, sm, smbuf, tps, tpbuf, ssem, rsem, lsem) = refs
     nf, nc, nt, hl = dims
     tok, width = hid.shape
@@ -374,6 +374,14 @@
         z[i * 256 : (i + 1) * 256, :] = zz * sg
         zd[i * 256 : (i + 1) * 256, :] = sg * (1.0 + zz * (1.0 - sg))
 
+    pass_weights(3)
+    get_weights(3)
+    get_cot.wait()
+    wo = weights(off[3], off[4])
+    for i in range(tok // 256):
+        rows = slice(i * 256, (i + 1) * 256)
+        ggate[rows, :] = mm(cot[rows, :], wo).astype(BF16)
+
     dec_spread = []
     for k in range(1, nc):
         dec_copies[k - 1].wait_recv()
@@ -401,31 +409,13 @@
         mixed[rows, :] = mix
         gt = mix * z[rows, :]
         gated[rows, :] = gt
-        st[0, :, rows] = mm_nt(ones8, (gt * gt).astype(BF16))[0:1]
-    s_copies = [remote(st.at[0], stbuf.at[0, k - 1], tx(k)) for k in range(1, nt)]
-
-    pass_weights(3)
-    get_weights(3)
-    get_cot.wait()
-    wo = weights(off[3], off[4])
-    for i in range(nb):
-        rows = slice(i * TB, (i + 1) * TB)
-        gg = mm(cot[rows, :], wo).astype(BF16)
-        ggate[rows, :] = gg
-        st[1, :, rows] = mm_nt(ones8, (gg.astype(F32) * gain_gate * gated[rows, :]).astype(BF16))[0:1]
-    t_copies = [remote(st.at[1], stbuf.at[1, k - 1], tx(k)) for k in range(1, nt)]
+        st[0:1, rows] = mm_nt(ones8, (gt * gt).astype(BF16))[0:1]
+        gl = gt * gain_gate
+        glow[rows, :] = gl.astype(BF16)
+        st[1:2, rows] = mm_nt(ones8, (ggate[rows, :].astype(F32) * gl).astype(BF16))[0:1]
+    st_copies = [remote(st, stbuf.at[k - 1], tx(k)) for k in range(1, nt)]
     total_inner = inner * nt
     pick = (iota((8, 128), 0) == 0).astype(F32).astype(BF16)
-
-    def row_total(which, copies):
-        total = st[which]
-        for k in range(1, nt):
-            copies[k - 1].wait_recv()
-            total = total + stbuf[which, k - 1]
-        return total
-
-    r_row = lax.rsqrt(row_total(0, s_copies) * (1.0 / total_inner) + EPS)
-    r_cols = exact_right(jnp.broadcast_to(r_row, (8, tok)), pick, mm_tn)
 
     is_mid = (t > 0) & (t < nt - 1)
     is_end = (t == 0) | (t == nt - 1)
@@ -497,7 +487,7 @@
     local_count[0] += 2 * pieces
 
     def out_done(p, rows, both):
-        out_v[rows, :] = (hid[rows, :].astype(F32) + both.astype(F32)).astype(BF16)
+        out_v[rows, :] = (hid[rows, :].astype(F32) + both.astype(F32) * r_cols[rows, 0:1]).astype(BF16)
         result(result_ids + p, out_v, out_h, pl.ds(p * PR, PR)).start()
 
     def head_done(p, rows, both):
@@ -527,10 +517,25 @@
 
     for i in range(nb):
         rows = slice(i * TB, (i + 1) * TB)
-        gl = (gated[rows, :] * r_cols[rows, 0:1] * gain_gate).astype(BF16)
-        glow[rows, :] = gl
-        ob[rows, :] = mm_nt(gl, wo).astype(BF16)
+        ob[rows, :] = mm_nt(glow[rows, :], wo).astype(BF16)
         line_o.begin(range(i * TB // PR, (i + 1) * TB // PR))
+
+    def tp_order(own, box):
+        total = None
+        for k in range(nt):
+            part = jnp.where(t == k, own, 0.0)
+            for j in range(1, nt):
+                part = jnp.where(lax.rem(t + nt - j, nt) == k, box[j - 1].astype(F32), part)
+            total = part if total is None else total + part
+        return total
+
+    for copy in st_copies:
+        copy.wait_recv()
+    both = tp_order(st[...], stbuf)
+    r_row = lax.rsqrt(both[0:1, :] * (1.0 / total_inner) + EPS)
+    q_row = r_row * r_row * r_row * both[1:2, :] * (-1.0 / total_inner)
+    r_cols[...] = exact_right(jnp.broadcast_to(r_row, (8, tok)), pick, mm_tn)
+    q_cols = exact_right(jnp.broadcast_to(q_row, (8, tok)), pick, mm_tn)
 
     block = 384
     per = block // rows_w
@@ -539,12 +544,6 @@
         for s in range(per):
             gw16[b * per + s, :, lo:hi] = value[s * rows_w : (s + 1) * rows_w].astype(BF16)
 
-    for b in range(width // block):
-        cols = slice(b * block, (b + 1) * block)
-        store_grads(b, off[3], off[4], mm_tn(cot[:, cols], glow[...]))
-
-    q_row = r_row * r_row * r_row * row_total(1, t_copies) * (-1.0 / total_inner)
-    q_cols = exact_right(jnp.broadcast_to(q_row, (8, tok)), pick, mm_tn)
     acc_gain = jnp.zeros((1, inner), F32)
     acc_skip = jnp.zeros((1, inner), F32)
     for i in range(nb):
@@ -552,7 +551,9 @@
         r = r_cols[rows, 0:1]
         gt = gated[rows, :]
         gg = ggate[rows, :].astype(F32)
-        acc_gain = acc_gain + jnp.sum(gg * gt * r, axis=0, keepdims=True)
+        ghat = gt * r
+        glow[rows, :] = (ghat * gain_gate).astype(BF16)
+        acc_gain = acc_gain + jnp.sum(gg * ghat, axis=0, keepdims=True)
         ggated = gg * gain_gate * r + gt * q_cols[rows, 0:1]
         dm = ggated * z[rows, :]
         gall[rows, off[2] :] = (ggated * mixed[rows, :] * zd[rows, :]).astype(BF16)
@@ -609,6 +610,7 @@
     for b in range(width // block):
         cols = slice(b * block, (b + 1) * block)
         store_grads(b, off[2], off[3], mm_tn(nl[16:, cols], gall[:, off[2] :]))
+        store_grads(b, off[3], off[4], mm_tn(cot[:, cols], glow[...]))
     grads1 = send_grads(1)
 
     for i in range(nb):
@@ -795,18 +797,9 @@
     bcs[...] = got[:, :xo].astype(BF16)
     bc_copies = [remote(bcs, bcbuf.at[k - 1], tx(k)) for k in range(1, nt)]
     pump(PUMP[6][5])
-    def tp_order(own, box, first):
-        total = None
-        for k in range(nt):
-            part = jnp.where(t == k, own, 0.0)
-            for j in range(1, nt):
-                part = jnp.where(lax.rem(t + nt - j, nt) == k, box[first + j - 1].astype(F32), part)
-            total = part if total is None else total + part
-        return total
-
     for copy in tp_copies:
         copy.wait_recv()
-    got = tp_order(tps[...], tpbuf, 0)
+    got = tp_order(tps[...], tpbuf)
     small[...] = sm[2]
     for k in range(width // 128):
         small[0:1, k * 128 : (k + 1) * 128] = got[k : k + 1, :]
@@ -815,7 +808,7 @@
     pump(PUMP[6][6])
     for copy in bc_copies:
         copy.wait_recv()
-    gwbc[...] = tp_order(bcs[...].astype(F32), bcbuf, 0)
+    gwbc[...] = tp_order(bcs[...].astype(F32), bcbuf)
     keep(gwbc, gwbc_h)
     pump(len(todo))
 
@@ -951,10 +944,11 @@
         "mixed": ((tok, inner), F32),
         "dmix": ((tok, inner), F32),
         "dy": ((tok, inner), BF16),
-        "st": ((2, 1, tok), F32),
-        "stbuf": ((2, nt - 1, 1, tok), F32),
+        "st": ((2, tok), F32),
+        "stbuf": ((nt - 1, 2, tok), F32),
         "gall": ((tok, p2 + inner), BF16),
         "glow": ((tok, inner), BF16),
+        "r_cols": ((tok, 128), F32),
         "ob": ((tok, width), BF16),
         "oin": ((pieces, PR, width), BF16),
         "oex": ((pieces, PR, width), BF16),

time: 85.4 us -> 81.6 us (0.956)
  Pallas kernels: 84.4 us -> 80.6 us
    pallas_call x1, Pallas kernels: 81.5 us -> 77.7 us  [per_device(): pl.pallas_call(partial(mixer_kernel, (nf, nc, nt, hl)), out_shape=(bf16(t...]
where the time goes in v4:
time: 81.6 us; the launch traced here: 81.4 us
  Pallas kernels  80.6 us (99%)
  between operations  0.84 us (1%)
    pallas_call x1, Pallas kernels, per_device(): pl.pallas_call(partial(mixer_kernel, (nf, nc, nt, hl)), out_shape=(bf16(t...  77.7 us
    pallas_call x1, Pallas kernels, per_device(): pl.pallas_call(partial(finish_kernel, (hl, xo)), out_shape=finals, in_spe...  2.88 us

profile of v4, /device:TPU:0, one launch (start us, length us, event | category | flops | bytes accessed | tf_op | source)
XLA Modules:
  0.0 81.4 jit_solution(3084995431267097481)
XLA Ops:
  0.7 77.7 %shard_map.254 = (bf16[512,768]{1,0:T(8,128)(2,1)}, f32[512,768]{1,0:T(8,128)}, f32[96,384]{1,0:T(8,128)}, f32[96,384]{1,0:T(8,128)}, f32[96,128]{1,0:T(8,128)},...) custom-call(s32[1,4]{1,0:T(1,128)} %refs_0_.1, f32[768]{0:T(1024)} %refs_1_.1, bf16[6,2,96]{2,1,0:T(2,128)(2,1)} %bitcast.5, ...), custom_call_target="tpu_custom_call" | custom-call | tf_op jit(solution)/shard_map/pallas_call | solution.py:985
  78.4 2.9 %shard_map.255 = (f32[512,768]{1,0:T(8,128)}, bf16[512,768]{1,0:T(8,128)(2,1)}, f32[96,384]{1,0:T(8,128)}, f32[96,384]{1,0:T(8,128)}, f32[96,128]{1,0:T(8,128)},...) custom-call(f32[96,128]{1,0:T(8,128)} %get-tuple-element.36.gdt_h, ...), custom_call_target="tpu_custom_call" | custom-call | tf_op jit(solution)/shard_map/pallas_call | solution.py:1009

commit v5 on v4

--- a/solution.py
+++ b/solution.py
@@ -281,20 +281,9 @@
     dte[...] = mm(step.astype(BF16), spread).astype(BF16)
     tol[...] = mm(to_end.astype(BF16), spread).astype(BF16)
     pass_weights(1)
-    rea[...] = mm(reach.astype(BF16), spread).astype(BF16)
 
     b16 = low[:, 0:state_n]
     c16 = low[:, state_n:xo]
-
-    def mix_mask(i):
-        same = seg_col(i * TB, TB) == seg_row
-        return same & (iota((TB, 1), 0) + i * TB != place_row)
-
-    for i in range(nb):
-        lo, hi = i * TB, (i + 1) * TB
-        mask = mix_mask(i)
-        gm[lo:hi, :] = jnp.where(mask, mm_nt(c16[lo:hi], b16), 0.0)
-        gmt[lo:hi, :] = jnp.where(mask, mm_nt(b16[lo:hi], c16), 0.0)
 
     get_weights(1)
     w_part = weights(off[1], off[2])
@@ -321,6 +310,20 @@
         forward = lax.rem(c + k, nc) > c
         state_copies.append(remote(s16.at[:, half_of(forward)], sbuf.at[k - 1], cx(k)))
 
+    rea[...] = mm(reach.astype(BF16), spread).astype(BF16)
+
+    def mix_mask(i):
+        same = seg_col(i * TB, TB) == seg_row
+        return same & (iota((TB, 1), 0) + i * TB != place_row)
+
+    for i in range(nb):
+        lo, hi = i * TB, (i + 1) * TB
+        mask = mix_mask(i)
+        gm[lo:hi, :] = jnp.where(mask, mm_nt(c16[lo:hi], b16), 0.0)
+        gmt[lo:hi, :] = jnp.where(mask, mm_nt(b16[lo:hi], c16), 0.0)
+
+    pass_weights(2)
+
     local = iota((TB, TB), 0)
     below = local > iota((TB, TB), 1)
     above = local < iota((TB, TB), 1)
@@ -337,8 +340,6 @@
 
     for i in range(nb):
         lo, hi = i * TB, (i + 1) * TB
-        if i == 2:
-            pass_weights(2)
         g_diag = gm[lo:hi, lo:hi]
         g_low = jnp.where(below, g_diag, 0.0)
         g_up = jnp.where(above, g_diag, 0.0)

time: 81.6 us -> 81.6 us (level)
  no operation moved by 1% of the time
where the time goes in v5:
time: 81.6 us; the launch traced here: 81.4 us
  Pallas kernels  80.5 us (99%)
  between operations  0.84 us (1%)
    pallas_call x1, Pallas kernels, per_device(): pl.pallas_call(partial(mixer_kernel, (nf, nc, nt, hl)), out_shape=(bf16(t...  77.7 us
    pallas_call x1, Pallas kernels, per_device(): pl.pallas_call(partial(finish_kernel, (hl, xo)), out_shape=finals, in_spe...  2.88 us

profile of v5, /device:TPU:0, one launch (start us, length us, event | category | flops | bytes accessed | tf_op | source)
XLA Modules:
  0.0 81.4 jit_solution(2160444206422326574)
XLA Ops:
  0.7 77.7 %shard_map.254 = (bf16[512,768]{1,0:T(8,128)(2,1)}, f32[512,768]{1,0:T(8,128)}, f32[96,384]{1,0:T(8,128)}, f32[96,384]{1,0:T(8,128)}, f32[96,128]{1,0:T(8,128)},...) custom-call(s32[1,4]{1,0:T(1,128)} %refs_0_.1, f32[768]{0:T(1024)} %refs_1_.1, bf16[6,2,96]{2,1,0:T(2,128)(2,1)} %bitcast.5, ...), custom_call_target="tpu_custom_call" | custom-call | tf_op jit(solution)/shard_map/pallas_call | solution.py:986
  78.3 2.9 %shard_map.255 = (f32[512,768]{1,0:T(8,128)}, bf16[512,768]{1,0:T(8,128)(2,1)}, f32[96,384]{1,0:T(8,128)}, f32[96,384]{1,0:T(8,128)}, f32[96,128]{1,0:T(8,128)},...) custom-call(f32[96,128]{1,0:T(8,128)} %get-tuple-element.36.gdt_h, ...), custom_call_target="tpu_custom_call" | custom-call | tf_op jit(solution)/shard_map/pallas_call | solution.py:1010
